TPU v7x, 32 devices: a whole 2x2x4 slice. The times are simulated.
32 devices in a mesh: cls: 8 (over y, x, core), batch: 4 (over z).
Axes of the slice: x: 2, y: 2, z: 4, core: 2. Of those that a mesh axis runs over, the one named last changes fastest.
Arguments:
- features: bfloat16 [4096, 1024], P('batch'), may hold values from -6 to 6
- head_weight: bfloat16 [1024, 1024], P('cls'), may hold values from -0.1875 to 0.1875
- inliers: bfloat16 [8192, 1024], P('cls'), may hold values from -2.5 to 2.5
- outliers: bfloat16 [8192, 1024], P('cls'), may hold values from -2.5 to 2.5
- inlier_counts: int32 [8192], P('cls'), may hold values from 1 to 9
- outlier_counts: int32 [8192], P('cls'), may hold values from 1 to 9
- labels: int32 [4096], P('batch'), may hold values from 0 to 1
Outputs:
- energy: float32 [4096], P('batch')
- head_grad: float32 [1024, 1024], P('cls')
All inputs are finite; a program needn't handle non-finite values.
Results may differ from a plain program's by a relative error of at most 0.0076.
The roundings to bfloat16 on the way count: a program that leaves them out, or rounds other values in their place, can miss the bound.
Values may be sent and summed in bfloat16 or wider, within the bound.
No kernel may reach another device: no remote copies, remote signals or barrier semaphores. Data moves between devices by JAX's collectives and lax.ppermute only.
A program may use at most 64 MiB of HBM per device.

v0:
```python
import jax
import jax.numpy as jnp
from jax import lax
from jax.sharding import PartitionSpec as P

beta = 2.0


def score_rows(queries, patterns, counts):
    log_counts = jnp.log(counts.astype(jnp.float32))
    return (
        beta * jnp.dot(queries, patterns.T, preferred_element_type=jnp.float32)
        + log_counts[None, :]
    )


def split_parts(values):
    high_part = values.astype(jnp.bfloat16)
    low_part = (values - high_part.astype(jnp.float32)).astype(jnp.bfloat16)
    return (high_part, low_part)


def outer_rows(columns, high_part, low_part):
    first = jnp.einsum("qf,qd->fd", columns, high_part, preferred_element_type=jnp.float32)
    return first + jnp.einsum("qf,qd->fd", columns, low_part, preferred_element_type=jnp.float32)


def body(features, head_weight, inliers, outliers, inlier_counts, outlier_counts, labels):
    columns = features
    queries = jnp.dot(
        columns,
        lax.all_gather(head_weight, "cls", axis=0, tiled=True),
        preferred_element_type=jnp.float32,
    ).astype(jnp.bfloat16)
    in_scores = score_rows(queries, inliers, inlier_counts)
    out_scores = score_rows(queries, outliers, outlier_counts)
    in_top, out_top = lax.pmax((jnp.max(in_scores, axis=1), jnp.max(out_scores, axis=1)), "cls")
    in_expon = jnp.exp(in_scores - in_top[:, None])
    out_expon = jnp.exp(out_scores - out_top[:, None])
    in_total, out_total = lax.psum((jnp.sum(in_expon, axis=1), jnp.sum(out_expon, axis=1)), "cls")
    in_sum = jnp.dot(in_expon.astype(jnp.bfloat16), inliers, preferred_element_type=jnp.float32)
    out_sum = jnp.dot(out_expon.astype(jnp.bfloat16), outliers, preferred_element_type=jnp.float32)
    energy = (in_top + jnp.log(in_total) - (out_top + jnp.log(out_total))) / beta
    label_sign = 2.0 * labels.astype(jnp.float32) - 1.0
    slope_term = -label_sign * jax.nn.sigmoid(-label_sign * energy)
    query_grad = slope_term[:, None] * (in_sum / in_total[:, None] - out_sum / out_total[:, None])
    grad_high, grad_low = split_parts(query_grad)
    columns = features
    partial_value = lax.psum_scatter(
        outer_rows(columns, grad_high, grad_low), "cls", scatter_dimension=0, tiled=True
    )
    head_grad = lax.psum(partial_value, "batch")
    return (energy, head_grad)


def solution(mesh):
    placed = (
        P("batch", None),
        P("cls", None),
        P("cls", None),
        P("cls", None),
        P("cls"),
        P("cls"),
        P("batch"),
    )
    return jax.shard_map(
        body, mesh=mesh, in_specs=placed, out_specs=(P("batch"), P("cls", None)), check_vma=False
    )
```

profile of v0, /device:TPU:0, one launch (start us, length us, event | category | flops | bytes accessed | tf_op | source)
XLA Modules:
  0.0 203.2 jit_solution(14456666442789482762)
XLA Ops:
  7.2 0.0 copy-start
  7.2 0.0 all-gather.2.cloned.1.call-start
  7.2 0.7 all-gather.2.cloned.1.call-update
  7.9 0.0 reduce-scatter.2.cloned.1.call-start
  8.0 0.7 convert_log_fusion.1
  8.7 0.7 convert_log_fusion
  9.3 31.1 %all-gather.2.cloned.1.call-done = bf16[1024,1024]{1,0:T(8,128)(2,1)} async-done(((bf16[128,1024]{1,0:T(8,128)(2,1)}), bf16[1024,1024]{1,0:T(8,128)(2,1)}) %all-gather.2.cloned.1.call-update) | async-done | bytes 2097168 | tf_op jit(solution)/shard_map/all_gather | solution.py:32
  40.4 0.0 copy-done
  40.4 0.0 copy-start.4
  40.4 4.1 %convolution_convert_fusion = bf16[1024,1024]{1,0:T(8,128)(2,1)S(1)} fusion(bf16[1024,1024]{1,0:T(8,128)(2,1)S(1)} %copy-done, bf16[1024,1024]{1,0:T(8,128)(2,1)} %all-gather.2.cloned.1.call-done), kind=kOutput, calls=%fused_computation.22 | convolution fusion | flops 2148532224 | bytes 6291456 | tf_op jit(solution)/shard_map/dot_general | solution.py:30
  44.5 0.0 copy-done.4
  44.5 0.0 copy-start.5
  44.5 4.3 %fusion.1 = (f32[1024]{0:T(1024)S(1)}, f32[1024,1024]{0,1:T(8,128)}) fusion(f32[1024]{0:T(1024)S(1)} %convert_log_fusion, bf16[1024,1024]{1,0:T(8,128)(2,1)S(1)} %convolution_convert_fusion, bf16[1024,1024]{1,0:T(8,128)(2,1)S(1)} %copy-done.4), kind=kOutput, calls=%fused_computation.8 | convolution fusion | flops 2150628352 | bytes 8396800 | tf_op jit(solution)/shard_map/dot_general | solution.py:12
  48.8 0.0 copy-done.5
  48.8 4.3 %fusion = (f32[1024]{0:T(1024)S(1)}, f32[1024,1024]{0,1:T(8,128)}) fusion(f32[1024]{0:T(1024)S(1)} %convert_log_fusion.1, bf16[1024,1024]{1,0:T(8,128)(2,1)S(1)} %convolution_convert_fusion, bf16[1024,1024]{1,0:T(8,128)(2,1)S(1)} %copy-done.5), kind=kOutput, calls=%fused_computation.7 | convolution fusion | flops 2150628352 | bytes 8396800 | tf_op jit(solution)/shard_map/dot_general | solution.py:12
  53.2 13.3 %all-reduce.1 = (f32[1024]{0:T(1024)S(1)}, f32[1024]{0:T(1024)S(1)}) all-reduce(f32[1024]{0:T(1024)S(1)} %get-tuple-element.10, f32[1024]{0:T(1024)S(1)} %get-tuple-element.12), channel_id=1, replica_groups=mesh['cls'=8,'batch'=4] {'cls'}, use_global_device_ids=true, to_apply=%region_5.0 | all-reduce | flops 2048 | bytes 16384 | tf_op jit(solution)/shard_map/pmax | solution.py:37
  66.5 0.0 copy-start.1
  66.5 0.0 copy-start.2
  66.5 7.5 %fusion.6 = f32[1024,1024]{1,0:T(8,128)} fusion(bf16[1024,1024]{1,0:T(8,128)(2,1)} %param.10, f32[1024,1024]{0,1:T(8,128)} %get-tuple-element.11, f32[1024]{0:T(1024)S(1)} %get-tuple-element.6, f32[1024]{0:T(1024)S(1)} %convert_log_fusion), kind=kOutput, calls=%fused_computation.13 | convolution fusion | flops 2151677952 | bytes 10493952 | tf_op jit(solution)/shard_map/dot_general | solution.py:42
  74.0 0.0 copy-done.1
  74.0 0.0 copy-done.2
  74.0 0.0 copy-start.3
  74.0 1.9 fusion.3
  75.9 12.2 %all-reduce = (f32[1024]{0:T(1024)S(1)}, f32[1024]{0:T(1024)S(1)}) all-reduce(f32[1024]{0:T(1024)S(1)} %get-tuple-element.15, f32[1024]{0:T(1024)S(1)} %get-tuple-element.14), channel_id=1, replica_groups=mesh['cls'=8,'batch'=4] {'cls'}, use_global_device_ids=true, to_apply=%region_7.0 | all-reduce | flops 2048 | bytes 16384 | tf_op jit(solution)/shard_map/psum | solution.py:40
  88.2 0.0 copy-done.3
  88.2 0.6 divide_multiply_fusion
  88.8 6.9 %subtract_multiply_fusion = f32[1024,1024]{1,0:T(8,128)S(1)} fusion(f32[1024,1024]{1,0:T(8,128)} %fusion.6, f32[1024]{0:T(1024)S(1)} %get-tuple-element.4, f32[1024]{0:T(1024)S(1)} %get-tuple-element.5, f32[1024]{0:T(1024)S(1)} %get-tuple-element.8, bf16[1024,1024]{1,0:T(8,128)(2,1)} %param.9, f32[1024,1024]{0,1:T(8,128)} %get-tuple-element.13, ...), kind=kOutput, calls=%fused_computation.2 | convolution fusion | flops 2155872256 | bytes 14700544 | tf_op jit(solution)/shard_map/dot_general | solution.py:41
  95.7 2.4 %fusion.20 = f32[1024,1024]{1,0:T(8,128)S(1)} fusion(bf16[1024,1024]{1,0:T(8,128)(2,1)S(1)} %copy-done, f32[1024,1024]{1,0:T(8,128)S(1)} %subtract_multiply_fusion), kind=kOutput, calls=%fused_computation.24 | convolution fusion | flops 2148532224 | bytes 10485760 | tf_op jit(solution)/shard_map/qf,qd->fd/dot_general | solution.py:24
  98.1 4.3 %add_bitcast_fusion = f32[1024,1024]{0,1:T(8,128)} fusion(f32[1024,1024]{1,0:T(8,128)S(1)} %fusion.20, bf16[1024,1024]{1,0:T(8,128)(2,1)S(1)} %copy-done, f32[1024,1024]{1,0:T(8,128)S(1)} %subtract_multiply_fusion), kind=kOutput, calls=%fused_computation | convolution fusion | flops 2152726528 | bytes 14680064 | tf_op jit(solution)/shard_map/qf,qd->fd/dot_general | solution.py:25
  102.4 0.0 reduce-scatter.2.cloned.1.call-update
  102.4 0.0 all-reduce.4.cloned.1.call-start
  102.4 51.3 %reduce-scatter.2.cloned.1.call-done = f32[128,1024]{0,1:T(8,128)} async-done(((f32[1024,1024]{0,1:T(8,128)}), f32[128,1024]{0,1:T(8,128)}) %reduce-scatter.2.cloned.1.call-update) | async-done | bytes 524304 | tf_op jit(solution)/shard_map/reduce_scatter | solution.py:49
  153.7 0.0 all-reduce.4.cloned.1.call-update
  153.7 40.9 %all-reduce.4.cloned.1.call-done = f32[128,1024]{0,1:T(8,128)} async-done(((f32[128,1024]{0,1:T(8,128)}), f32[128,1024]{0,1:T(8,128)}) %all-reduce.4.cloned.1.call-update) | async-done | bytes 524304 | tf_op jit(solution)/shard_map/psum | solution.py:52
  194.7 2.0 %copy.9 = f32[128,1024]{1,0:T(8,128)} copy(f32[128,1024]{0,1:T(8,128)} %all-reduce.4.cloned.1.call-done) | data formatting | bytes 1048576
Async XLA Ops:
  7.2 33.2 %copy-start = (bf16[1024,1024]{1,0:T(8,128)(2,1)S(1)}, bf16[1024,1024]{1,0:T(8,128)(2,1)}, u32[]{:S(2)}) copy-start(bf16[1024,1024]{1,0:T(8,128)(2,1)} %param.7) | copy-start | bytes 6291460
  7.2 33.2 %all-gather.2.cloned.1.call-start = ((), (), s32[]{:S(2)}) async-start(), calls=%async_computation.1 | async-start | bytes 2359296 | tf_op jit(solution)/shard_map/all_gather | solution.py:32
  7.9 145.8 %reduce-scatter.2.cloned.1.call-start = ((), (), s32[]{:S(2)}) async-start(), calls=%async_computation.2 | async-start | bytes 4718592 | tf_op jit(solution)/shard_map/reduce_scatter | solution.py:49
  40.4 4.1 %copy-start.4 = (bf16[1024,1024]{1,0:T(8,128)(2,1)S(1)}, bf16[1024,1024]{1,0:T(8,128)(2,1)}, u32[]{:S(2)}) copy-start(bf16[1024,1024]{1,0:T(8,128)(2,1)} %param.10) | copy-start | bytes 6291460
  44.5 4.3 %copy-start.5 = (bf16[1024,1024]{1,0:T(8,128)(2,1)S(1)}, bf16[1024,1024]{1,0:T(8,128)(2,1)}, u32[]{:S(2)}) copy-start(bf16[1024,1024]{1,0:T(8,128)(2,1)} %param.9) | copy-start | bytes 6291460
  66.5 7.5 %copy-start.1 = (f32[1024,1024]{0,1:T(8,128)S(1)}, f32[1024,1024]{0,1:T(8,128)}, u32[]{:S(2)}) copy-start(f32[1024,1024]{0,1:T(8,128)} %get-tuple-element.13) | copy-start | bytes 12582916
  66.5 7.5 %copy-start.2 = (f32[1024,1024]{0,1:T(8,128)S(1)}, f32[1024,1024]{0,1:T(8,128)}, u32[]{:S(2)}) copy-start(f32[1024,1024]{0,1:T(8,128)} %get-tuple-element.11) | copy-start | bytes 12582916
  74.0 14.2 %copy-start.3 = (s32[1024]{0:T(1024)S(1)}, s32[1024]{0:T(1024)}, u32[]{:S(2)}) copy-start(s32[1024]{0:T(1024)} %param.13) | copy-start | bytes 12292
  102.4 92.3 %all-reduce.4.cloned.1.call-start = ((), (), s32[]{:S(2)}) async-start(), calls=%async_computation.3 | async-start | bytes 1048576 | tf_op jit(solution)/shard_map/psum | solution.py:52
Sparse Core Ops, SparseCore 0:
  9.9 30.4 all-gather.1
  102.5 51.1 reduce-scatter.1
  156.1 38.5 all-reduce.3
where the time goes:
time: 204 us; the launch traced here: 203 us
  waiting for transfers between devices  124 us (61%)
  matrix products  33.8 us (17%)
  blocking collectives  25.5 us (12%)
  between operations  13.8 us (7%)
  other arithmetic  3.94 us (2%)
  local copies, waits for them, and re-layouts  2.07 us (1%)
    reduce_scatter x1, waiting for transfers between devices, body(): lax.psum_scatter(outer_rows(columns, grad_high, grad_low), 'cls', scatter...  51.3 us
    psum x1, waiting for transfers between devices, body(): head_grad = lax.psum(partial_value, 'batch')  40.9 us
    all_gather x1, waiting for transfers between devices, body(): lax.all_gather(head_weight, 'cls', axis=0, tiled=True)  31.1 us
    pmax x1, blocking collectives, body(): lax.pmax((jnp.max(in_scores, axis=1), jnp.max(out_scores, axis=1)), 'cls')  13.3 us
    psum x1, blocking collectives, body(): lax.psum((jnp.sum(in_expon, axis=1), jnp.sum(out_expon, axis=1)), 'cls')  12.2 us
    dot_general x2, matrix products, score_rows(): jnp.dot(queries, patterns.T, preferred_element_type=jnp.float32)  8.65 us
    dot_general x1, matrix products, body(): jnp.dot(out_expon.astype(jnp.bfloat16), outliers, preferred_element_type=...  7.48 us
    dot_general x1, matrix products, body(): jnp.dot(in_expon.astype(jnp.bfloat16), inliers, preferred_element_type=jn...  6.85 us
  transfers between devices with their start and end apart: 3, of which 3 were waited for; matrix products, arithmetic and copies ran while one was open for 1% of the time, Pallas kernels for 0%

commit v1 on v0

v1 whole, which is shorter than its diff:
```python
import functools

import jax
import jax.numpy as jnp
from jax import lax
from jax.experimental import pallas as pl
from jax.experimental.pallas import tpu as pltpu
from jax.sharding import PartitionSpec as P

beta = 2.0
BF = jnp.bfloat16
F32 = jnp.float32


def orders(bits):
    turn = len(bits) // 2
    return bits, bits[turn:] + bits[:turn]


def gather_masks(order):
    masks = [0, 1]
    for bit in order:
        masks = masks + [mask ^ (1 << bit) for mask in masks]
    return masks


def scatter_masks(order):
    masks = [0]
    for bit in reversed(order):
        masks = [mask ^ (1 << bit) for mask in masks] + masks
    return masks


def by_core(core, first, second):
    return jnp.where(core == 0, jnp.array(first, jnp.int32), jnp.array(second, jnp.int32))


def cls_swap(value, n, bit_of):
    return lax.ppermute(value, "cls", [(i, i ^ (1 << bit_of[i & 1])) for i in range(n)])


def batch_swap(value, n, depth, bit_of):
    pairs = []
    for i in range(n):
        for j in range(depth):
            pairs.append((i * depth + j, i * depth + (j ^ (1 << bit_of[i & 1]))))
    return lax.ppermute(value, ("cls", "batch"), pairs)


def turn_kernel(place_ref, features_ref, out_ref, turned_ref, *, n, rows):
    turned_ref[...] = features_ref[...].T
    for p in range(n):
        start = pl.multiple_of(place_ref[p] * rows, rows)
        out_ref[p * rows:(p + 1) * rows, :] = turned_ref[pl.ds(start, rows), :]


def turn_features(features, place, n):
    q, f = features.shape
    return pl.pallas_call(
        functools.partial(turn_kernel, n=n, rows=f // n),
        out_shape=jax.ShapeDtypeStruct((f, q), BF),
        in_specs=[pl.BlockSpec(memory_space=pltpu.SMEM), pl.BlockSpec(memory_space=pltpu.VMEM)],
        out_specs=pl.BlockSpec(memory_space=pltpu.VMEM),
        scratch_shapes=[pltpu.VMEM((f, q), BF)],
        compiler_params=pltpu.CompilerParams(vmem_limit_bytes=16 << 20),
        cost_estimate=pl.CostEstimate(flops=0, bytes_accessed=8 * q * f, transcendentals=0),
        name="turn",
    )(place, features)


def query_kernel(place_ref, features_ref, blocks_ref, out_ref, weight_ref, *, n, rows, tile):
    for p in range(n):
        start = pl.multiple_of(place_ref[p] * rows, rows)
        weight_ref[pl.ds(start, rows), :] = blocks_ref[p * rows:(p + 1) * rows, :]
    total = features_ref.shape[0]

    @pl.loop(0, total // tile)
    def _(i):
        part = pl.ds(pl.multiple_of(i * tile, tile), tile)
        out_ref[part, :] = jnp.dot(
            features_ref[part, :], weight_ref[...], preferred_element_type=F32
        ).astype(BF)


def half_queries(features, blocks, place, n):
    q, f = features.shape
    width = blocks.shape[1]
    return pl.pallas_call(
        functools.partial(query_kernel, n=n, rows=f // n, tile=256),
        out_shape=jax.ShapeDtypeStruct((q, width), BF),
        in_specs=[pl.BlockSpec(memory_space=pltpu.SMEM)] + [pl.BlockSpec(memory_space=pltpu.VMEM)] * 2,
        out_specs=pl.BlockSpec(memory_space=pltpu.VMEM),
        scratch_shapes=[pltpu.VMEM((f, width), BF)],
        compiler_params=pltpu.CompilerParams(vmem_limit_bytes=16 << 20),
        cost_estimate=pl.CostEstimate(flops=2 * q * f * width, bytes_accessed=4 * q * f, transcendentals=0),
        name="queries",
    )(place, features, blocks)


def to_rows(columns, width):
    r = columns[0].shape[0]
    lane = lax.broadcasted_iota(jnp.int32, (r, width), 1)
    mixed = jnp.broadcast_to(columns[0], (r, width))
    for i, column in enumerate(columns[1:], 1):
        mixed = jnp.where(lane == i, column, mixed)
    return mixed.T[: len(columns), :]


def score_kernel(core_ref, mine_ref, other_ref, in_ref, out_ref, in_counts_ref, out_counts_ref,
                 in_weights_ref, out_weights_ref, stats_ref, query_ref):
    half = mine_ref.shape[1]
    core = core_ref[0]
    query_ref[:, pl.ds(pl.multiple_of(core * half, half), half)] = mine_ref[...] * beta
    query_ref[:, pl.ds(pl.multiple_of((1 - core) * half, half), half)] = other_ref[...] * beta
    stats = []
    for patterns_ref, counts_ref, weights_ref in (
        (in_ref, in_counts_ref, in_weights_ref),
        (out_ref, out_counts_ref, out_weights_ref),
    ):
        scores = lax.dot_general(
            query_ref[...], patterns_ref[...], (((1,), (1,)), ((), ())), preferred_element_type=F32
        ) + jnp.log(counts_ref[...].astype(F32))
        top = jnp.max(scores, axis=1, keepdims=True)
        expon = jnp.exp(scores - top)
        weights_ref[...] = expon.astype(BF)
        stats += [top, jnp.sum(expon, axis=1, keepdims=True)]
    stats_ref[...] = to_rows(stats, 128)


def local_weights(core, mine, other, inliers, outliers, in_counts, out_counts):
    q, half = mine.shape
    d = inliers.shape[1]
    tile = 256
    row = lambda i, *_: (i, 0)
    whole = lambda i, *_: (0, 0)
    ins, outs = inliers.shape[0], outliers.shape[0]
    return pl.pallas_call(
        score_kernel,
        out_shape=(
            jax.ShapeDtypeStruct((q, ins), BF),
            jax.ShapeDtypeStruct((q, outs), BF),
            jax.ShapeDtypeStruct((4, q), F32),
        ),
        grid_spec=pltpu.PrefetchScalarGridSpec(
            num_scalar_prefetch=1,
            grid=(q // tile,),
            in_specs=[
                pl.BlockSpec((tile, half), row),
                pl.BlockSpec((tile, half), row),
                pl.BlockSpec((ins, d), whole),
                pl.BlockSpec((outs, d), whole),
                pl.BlockSpec((1, ins), whole),
                pl.BlockSpec((1, outs), whole),
            ],
            out_specs=[
                pl.BlockSpec((tile, ins), row),
                pl.BlockSpec((tile, outs), row),
                pl.BlockSpec((4, tile), lambda i, *_: (0, i)),
            ],
            scratch_shapes=[pltpu.VMEM((tile, d), BF)],
        ),
        compiler_params=pltpu.CompilerParams(vmem_limit_bytes=32 << 20),
        cost_estimate=pl.CostEstimate(
            flops=2 * q * d * (ins + outs), bytes_accessed=2 * d * (ins + outs), transcendentals=q * (ins + outs)
        ),
        name="scores",
    )(core, mine, other, inliers, outliers, in_counts, out_counts)


def merge(mine, other):
    rows = []
    for i in (0, 2):
        top = jnp.maximum(mine[i], other[i])
        rows += [top, mine[i + 1] * jnp.exp(mine[i] - top) + other[i + 1] * jnp.exp(other[i] - top)]
    return jnp.stack(rows)


def outer_kernel(scale_ref, in_ref, out_ref, turned_ref, send_ref, keep_ref, wide_ref):
    q = in_ref.shape[0]
    half = send_ref.shape[0]

    @pl.when(pl.program_id(0) == 0)
    def _():
        for i in range(2):
            wide_ref[i] = jnp.broadcast_to(scale_ref[i:i + 1, :], (128, q)).T

    copies = in_ref.shape[1] // 128
    in_scale = jnp.concatenate([wide_ref[0]] * copies, axis=1)
    out_scale = jnp.concatenate([wide_ref[1]] * copies, axis=1)
    grad = (in_scale * in_ref[...] - out_scale * out_ref[...]).astype(BF)
    send_ref[...] = jnp.dot(turned_ref[:half, :], grad, preferred_element_type=F32).astype(BF)
    keep_ref[...] = jnp.dot(turned_ref[half:, :], grad, preferred_element_type=F32)


def outer(scales, in_sum, out_sum, turned):
    q, d = in_sum.shape
    f = turned.shape[0]
    tile = 256
    column = lambda i: (0, i)
    whole = lambda i: (0, 0)
    return pl.pallas_call(
        outer_kernel,
        out_shape=(jax.ShapeDtypeStruct((f // 2, d), BF), jax.ShapeDtypeStruct((f // 2, d), F32)),
        grid=(d // tile,),
        in_specs=[
            pl.BlockSpec((2, q), whole),
            pl.BlockSpec((q, tile), column),
            pl.BlockSpec((q, tile), column),
            pl.BlockSpec((f, q), whole),
        ],
        out_specs=[pl.BlockSpec((f // 2, tile), column), pl.BlockSpec((f // 2, tile), column)],
        scratch_shapes=[pltpu.VMEM((2, q, 128), F32)],
        compiler_params=pltpu.CompilerParams(vmem_limit_bytes=32 << 20),
        cost_estimate=pl.CostEstimate(flops=2 * q * f * d, bytes_accessed=8 * q * d, transcendentals=0),
        name="outer",
    )(scales, in_sum, out_sum, turned)


def body(features, head_weight, inliers, outliers, inlier_counts, outlier_counts, labels):
    n = lax.axis_size("cls")
    depth = lax.axis_size("batch")
    me = lax.axis_index("cls")
    core = me & 1
    d = head_weight.shape[1]
    half = d // 2
    links = list(range(1, n.bit_length() - 1))
    first, second = orders(links)

    to_first, to_second = scatter_masks(first), scatter_masks(second)
    to_place = me ^ by_core(core, [m ^ 1 for m in to_second] + to_first, [m ^ 1 for m in to_first] + to_second)
    turned = turn_features(features, to_place, n)

    pieces = jnp.stack([head_weight[:, :half], head_weight[:, half:]])
    own = lax.dynamic_index_in_dim(pieces, core, 0, keepdims=False)
    give = lax.dynamic_index_in_dim(pieces, 1 - core, 0, keepdims=False)
    blocks = jnp.concatenate([own, cls_swap(give, n, (0, 0))])
    for bit_of in zip(first, second):
        blocks = jnp.concatenate([blocks, cls_swap(blocks, n, bit_of)])
    from_place = me ^ by_core(core, gather_masks(first), gather_masks(second))
    mine = half_queries(features, blocks, from_place, n)
    other = cls_swap(mine, n, (0, 0))

    in_weights, out_weights, stats = local_weights(
        core.reshape(1), mine, other, inliers, outliers,
        inlier_counts.reshape(1, -1), outlier_counts.reshape(1, -1),
    )
    whole = stats
    for bit in range(n.bit_length() - 1):
        whole = merge(whole, cls_swap(whole, n, (bit, bit)))
    in_sum = jnp.dot(in_weights, inliers, preferred_element_type=F32)
    out_sum = jnp.dot(out_weights, outliers, preferred_element_type=F32)
    energy = ((whole[0] + jnp.log(whole[1])) - (whole[2] + jnp.log(whole[3]))) / beta
    label_sign = 2.0 * labels.astype(F32) - 1.0
    slope = -label_sign * jax.nn.sigmoid(-label_sign * energy)
    scales = jnp.stack([
        slope * jnp.exp(stats[0] - whole[0]) / whole[1],
        slope * jnp.exp(stats[2] - whole[2]) / whole[3],
    ])
    send, keep = outer(scales, in_sum, out_sum, turned)

    total = keep + cls_swap(send, n, (0, 0)).astype(F32)
    for bit_of in zip(first, second):
        middle = total.shape[0] // 2
        got = cls_swap(total[:middle].astype(BF), n, bit_of)
        total = total[middle:] + got.astype(F32)
    for bit_of in zip(*orders(list(range(depth.bit_length() - 1)))):
        sent = total.astype(BF)
        total = sent.astype(F32) + batch_swap(sent, n, depth, bit_of).astype(F32)
    return energy, total


def solution(mesh):
    placed = (
        P("batch", None),
        P("cls", None),
        P("cls", None),
        P("cls", None),
        P("cls"),
        P("cls"),
        P("batch"),
    )
    return jax.shard_map(
        body, mesh=mesh, in_specs=placed, out_specs=(P("batch"), P("cls", None)), check_vma=False
    )
```

time: 204 us -> 86.2 us (0.42)
  waiting for transfers between devices: 124 us -> 44.7 us
  matrix products: 33.8 us -> 4.69 us
  blocking collectives: 25.5 us -> 0 us
  starting transfers between devices: 0.12 us -> 16.8 us
  Pallas kernels: 0 us -> 14.8 us
  between operations: 13.8 us -> 0.93 us
    reduce_scatter x1 -> x0, waiting for transfers between devices: 51.3 us -> none  [body(): lax.psum_scatter(outer_rows(columns, grad_high, grad_low), 'cls', scatter...]
    ppermute x0 -> x12, waiting for transfers between devices: none -> 44.7 us  [the longest x10 30.7 us: cls_swap(): lax.ppermute(value, 'cls', [(i, i ^ 1 << bit_of[i & 1]) for i in range(n)])]
    psum x1 -> x0, waiting for transfers between devices: 40.9 us -> none  [body(): head_grad = lax.psum(partial_value, 'batch')]
    all_gather x1 -> x0, waiting for transfers between devices: 31.1 us -> none  [body(): lax.all_gather(head_weight, 'cls', axis=0, tiled=True)]
    dot_general x7 -> x2, matrix products: 33.8 us -> 4.69 us  [the longest x1 2.36 us: body(): in_sum = jnp.dot(in_weights, inliers, preferred_element_type=F32)]
    ppermute x0 -> x12, starting transfers between devices: none -> 16.8 us  [the longest x10 12.4 us: cls_swap(): lax.ppermute(value, 'cls', [(i, i ^ 1 << bit_of[i & 1]) for i in range(n)])]
    pallas_call x0 -> x4, Pallas kernels: none -> 14.8 us  [the longest x1 6.94 us: local_weights(): pl.pallas_call(score_kernel, out_shape=(jax.ShapeDtypeStruct((q, ins), BF...]
    pmax x1 -> x0, blocking collectives: 13.3 us -> none  [body(): lax.pmax((jnp.max(in_scores, axis=1), jnp.max(out_scores, axis=1)), 'cls')]
  transfers between devices with their start and end apart: 3 -> 12, of which waited for: 3 -> 9; matrix products, arithmetic and copies ran while one was open for 1% -> 5% of each run, Pallas kernels for 0% -> 2%
where the time goes in v1:
time: 86.2 us; the launch traced here: 86 us
  waiting for transfers between devices  44.7 us (52%)
  starting transfers between devices  16.8 us (19%)
  Pallas kernels  14.8 us (17%)
  matrix products  4.69 us (5%)
  other arithmetic  2.94 us (3%)
  local copies, waits for them, and re-layouts  1.16 us (1%)
  between operations  0.93 us (1%)
    ppermute x10, waiting for transfers between devices, cls_swap(): lax.ppermute(value, 'cls', [(i, i ^ 1 << bit_of[i & 1]) for i in range(n)])  30.7 us
    ppermute x2, waiting for transfers between devices, batch_swap(): return lax.ppermute(value, ('cls', 'batch'), pairs)  14 us
    ppermute x10, starting transfers between devices, cls_swap(): lax.ppermute(value, 'cls', [(i, i ^ 1 << bit_of[i & 1]) for i in range(n)])  12.4 us
    pallas_call x1, Pallas kernels, local_weights(): pl.pallas_call(score_kernel, out_shape=(jax.ShapeDtypeStruct((q, ins), BF...  6.94 us
    ppermute x2, starting transfers between devices, batch_swap(): return lax.ppermute(value, ('cls', 'batch'), pairs)  4.37 us
    pallas_call x1, Pallas kernels, outer(): pl.pallas_call(outer_kernel, out_shape=(jax.ShapeDtypeStruct((f // 2, d),...  4.21 us
    pallas_call x1, Pallas kernels, half_queries(): pl.pallas_call(functools.partial(query_kernel, n=n, rows=f // n, tile=256...  2.36 us
    dot_general x1, matrix products, body(): in_sum = jnp.dot(in_weights, inliers, preferred_element_type=F32)  2.36 us
  transfers between devices with their start and end apart: 12, of which 9 were waited for; matrix products, arithmetic and copies ran while one was open for 5% of the time, Pallas kernels for 2%

profile of v1, /device:TPU:0, one launch (start us, length us, event | category | flops | bytes accessed | tf_op | source)
XLA Modules:
  0.0 86.0 jit_solution(4950388340691456120)
XLA Ops:
  0.6 0.0 copy-start.9
  0.6 1.0 %slice_bitcast_fusion = (bf16[1,128,512]{2,1,0:T(8,128)(2,1)S(1)}, bf16[1,128,512]{2,1,0:T(8,128)(2,1)S(1)}) fusion(bf16[128,1024]{1,0:T(8,128)(2,1)} %param.12), kind=kLoop, calls=%fused_computation.19 | loop fusion | bytes 524288 | tf_op jit(solution)/shard_map/stack | solution.py:233
  1.6 0.0 copy-start
  1.6 0.1 fusion.4
  1.8 0.6 collective-permute-start
  2.3 1.0 %collective-permute-done = bf16[128,512]{1,0:T(8,128)(2,1)S(1)} collective-permute-done((bf16[128,512]{1,0:T(8,128)(2,1)S(1)}, bf16[128,512]{1,0:T(8,128)(2,1)S(1)}, u32[]{:S(2)}, u32[]{:S(2)}) %collective-permute-start) | collective-permute-done | bytes 131104 | tf_op jit(solution)/shard_map/ppermute | solution.py:39
  3.3 2.9 %collective-permute-start.1 = (bf16[256,512]{1,0:T(8,128)(2,1)S(1)}, bf16[256,512]{1,0:T(8,128)(2,1)S(1)}, u32[]{:S(2)}, u32[]{:S(2)}) collective-permute-start(bf16[256,512]{1,0:T(8,128)(2,1)S(1)} %pad_maximum_fusion.2), channel_id=1, source_target_pairs={{0,8},{4,20},{8,0},{12,28},{16,24},{20,4},{24,16},{28,12},{1,9},{5... | collective-permute-start | bytes 786440 | tf_op jit(solution)/shard_map/ppermute | solution.py:39
  6.2 4.4 %collective-permute-done.1 = bf16[256,512]{1,0:T(8,128)(2,1)S(1)} collective-permute-done((bf16[256,512]{1,0:T(8,128)(2,1)S(1)}, bf16[256,512]{1,0:T(8,128)(2,1)S(1)}, u32[]{:S(2)}, u32[]{:S(2)}) %collective-permute-start.1) | collective-permute-done | bytes 262176 | tf_op jit(solution)/shard_map/ppermute | solution.py:39
  10.6 2.1 %collective-permute-start.2 = (bf16[512,512]{1,0:T(8,128)(2,1)S(1)}, bf16[512,512]{1,0:T(8,128)(2,1)}, u32[]{:S(2)}, u32[]{:S(2)}) collective-permute-start(bf16[512,512]{1,0:T(8,128)(2,1)S(1)} %pad_maximum_fusion.1), channel_id=1, source_target_pairs={{0,16},{4,12},{8,24},{12,4},{16,0},{20,28},{24,8},{28,20},{1,17},{... | collective-permute-start | bytes 1572872 | tf_op jit(solution)/shard_map/ppermute | solution.py:39
  12.8 7.3 %collective-permute-done.2 = bf16[512,512]{1,0:T(8,128)(2,1)} collective-permute-done((bf16[512,512]{1,0:T(8,128)(2,1)S(1)}, bf16[512,512]{1,0:T(8,128)(2,1)}, u32[]{:S(2)}, u32[]{:S(2)}) %collective-permute-start.2) | collective-permute-done | bytes 524320 | tf_op jit(solution)/shard_map/ppermute | solution.py:39
  20.0 1.1 %pad_maximum_fusion.blocks_ref = bf16[1024,512]{1,0:T(8,128)(2,1)S(1)} fusion(bf16[512,512]{1,0:T(8,128)(2,1)} %collective-permute-done.2, bf16[256,512]{1,0:T(8,128)(2,1)S(1)} %collective-permute-done.1, bf16[128,512]{1,0:T(8,128)(2,1)S(1)} %collective-permute-done, bf16[128,512]{1,0:T(8,128)(2,1)S(1)} %get-tuple-element.18), kind=kLoop, calls=%fused_computation.3 | loop fusion | flops 4194304 | bytes 2097152 | tf_op jit(solution)/shard_map/concatenate | solution.py:238
  21.2 0.0 copy-start.1
  21.2 0.0 copy-start.2
  21.2 0.0 copy-start.3
  21.2 2.4 %queries.1.mine_ref = bf16[1024,512]{1,0:T(8,128)(2,1)S(1)} custom-call(s32[8]{0:T(128)S(1)} %fusion.5.place_ref, bf16[1024,1024]{1,0:T(8,128)(2,1)S(1)} %copy-done, bf16[1024,512]{1,0:T(8,128)(2,1)S(1)} %pad_maximum_fusion.blocks_ref), custom_call_target="tpu_custom_call" | custom-call | flops 1073741824 | bytes 4194304 | tf_op jit(solution)/shard_map/queries/pallas_call | solution.py:88
  23.6 0.1 collective-permute-start.3
  23.6 2.6 %collective-permute-done.3.other_ref = bf16[1024,512]{1,0:T(8,128)(2,1)S(1)} collective-permute-done((bf16[1024,512]{1,0:T(8,128)(2,1)S(1)}, bf16[1024,512]{1,0:T(8,128)(2,1)S(1)}, u32[]{:S(2)}, u32[]{:S(2)}) %collective-permute-start.3) | collective-permute-done | bytes 1048608 | tf_op jit(solution)/shard_map/ppermute | solution.py:39
  26.3 0.0 copy-start.7
  26.3 0.0 copy-start.8
  26.3 6.9 %scores.1 = (bf16[1024,1024]{1,0:T(8,128)(2,1)S(1)}, bf16[1024,1024]{1,0:T(8,128)(2,1)S(1)}, f32[4,1024]{1,0:T(4,128)S(1)}) custom-call(s32[1]{0:T(128)} %bitcast.core_ref, bf16[1024,512]{1,0:T(8,128)(2,1)S(1)} %queries.1.mine_ref, bf16[1024,512]{1,0:T(8,128)(2,1)S(1)} %collective-permute-done.3.other_ref, bf16[1024,1024]{1,0:T(8,128)(2,1)S(1)} %copy-done.1, ...), custom_call_target="tpu_custom_call" | custom-call | flops 4294967296 | bytes 4194304 | tf_op jit(solution)/shard_map/scores/pallas_call | solution.py:137
  33.3 0.2 collective-permute-start.4
  33.5 1.3 %turn.1.turned_ref = bf16[1024,1024]{1,0:T(8,128)(2,1)S(1)} custom-call(s32[8]{0:T(128)S(1)} %fusion.6.place_ref, bf16[1024,1024]{1,0:T(8,128)(2,1)S(1)} %copy-done), custom_call_target="tpu_custom_call" | custom-call | bytes 8388608 | tf_op jit(solution)/shard_map/turn/pallas_call | solution.py:59
  34.8 0.0 collective-permute-done.4
  34.8 0.1 multiply_add_fusion.5
  34.9 2.1 %collective-permute-start.5 = (f32[4,1024]{1,0:T(4,128)S(1)}, f32[4,1024]{1,0:T(4,128)S(1)}, u32[]{:S(2)}, u32[]{:S(2)}) collective-permute-start(f32[4,1024]{1,0:T(4,128)S(1)} %pad_maximum_fusion.3), channel_id=1, source_target_pairs={{0,8},{4,12},{8,0},{12,4},{16,24},{20,28},{24,16},{28,20},{1,9},{5... | collective-permute-start | bytes 49160 | tf_op jit(solution)/shard_map/ppermute | solution.py:39
  36.9 2.4 %fusion.8.in_ref = f32[1024,1024]{1,0:T(8,128)S(1)} fusion(bf16[1024,1024]{1,0:T(8,128)(2,1)S(1)} %get-tuple-element.8, bf16[1024,1024]{1,0:T(8,128)(2,1)S(1)} %copy-done.1), kind=kOutput, calls=%fused_computation.45 | convolution fusion | flops 2147483648 | bytes 8388608 | tf_op jit(solution)/shard_map/dot_general | solution.py:250
  39.3 0.0 collective-permute-done.5
  39.4 1.6 %collective-permute-start.6 = (f32[4,1024]{1,0:T(4,128)S(1)}, f32[4,1024]{1,0:T(4,128)S(1)}, u32[]{:S(2)}, u32[]{:S(2)}) collective-permute-start(f32[4,1024]{1,0:T(4,128)S(1)} %pad_maximum_fusion.4), channel_id=1, source_target_pairs={{0,16},{4,20},{8,24},{12,28},{16,0},{20,4},{24,8},{28,12},{1,17},{... | collective-permute-start | bytes 49160 | tf_op jit(solution)/shard_map/ppermute | solution.py:39
  41.0 2.3 %fusion.9.out_ref = f32[1024,1024]{1,0:T(8,128)S(1)} fusion(bf16[1024,1024]{1,0:T(8,128)(2,1)S(1)} %get-tuple-element.9, bf16[1024,1024]{1,0:T(8,128)(2,1)S(1)} %copy-done.2), kind=kOutput, calls=%fused_computation.46 | convolution fusion | flops 2147483648 | bytes 8388608 | tf_op jit(solution)/shard_map/dot_general | solution.py:251
  43.3 0.0 collective-permute-done.6
  43.4 0.0 copy-start.6
  43.5 4.2 %outer.1 = (bf16[512,1024]{1,0:T(8,128)(2,1)S(1)}, f32[512,1024]{1,0:T(8,128)S(1)}) custom-call(f32[2,1024]{1,0:T(2,128)S(1)} %pad_maximum_fusion.5.scale_ref, f32[1024,1024]{1,0:T(8,128)S(1)} %fusion.8.in_ref, f32[1024,1024]{1,0:T(8,128)S(1)} %fusion.9.out_ref, bf16[1024,1024]{1,0:T(8,128)(2,1)S(1)} %turn.1.turned_ref), custom_call_target="tpu_custom_call" | custom-call | flops 2147483648 | bytes 8388608 | tf_op jit(solution)/shard_map/outer/pallas_call | solution.py:201
  47.7 0.1 collective-permute-start.7
  47.8 2.6 %collective-permute-done.7 = bf16[512,1024]{1,0:T(8,128)(2,1)S(1)} collective-permute-done((bf16[512,1024]{1,0:T(8,128)(2,1)S(1)}, bf16[512,1024]{1,0:T(8,128)(2,1)S(1)}, u32[]{:S(2)}, u32[]{:S(2)}) %collective-permute-start.7) | collective-permute-done | bytes 1048608 | tf_op jit(solution)/shard_map/ppermute | solution.py:39
  50.4 0.3 convert_add_fusion
  50.7 0.1 slice.146
  50.8 1.4 %collective-permute-start.8 = (bf16[256,1024]{1,0:T(8,128)(2,1)S(1)}, bf16[256,1024]{1,0:T(8,128)(2,1)S(1)}, u32[]{:S(2)}, u32[]{:S(2)}) collective-permute-start(bf16[256,1024]{1,0:T(8,128)(2,1)S(1)} %slice.146), channel_id=1, source_target_pairs={{0,8},{4,20},{8,0},{12,28},{16,24},{20,4},{24,16},{28,12},{1,9},{5... | collective-permute-start | bytes 1572872 | tf_op jit(solution)/shard_map/ppermute | solution.py:39
  52.2 7.8 %collective-permute-done.8 = bf16[256,1024]{1,0:T(8,128)(2,1)S(1)} collective-permute-done((bf16[256,1024]{1,0:T(8,128)(2,1)S(1)}, bf16[256,1024]{1,0:T(8,128)(2,1)S(1)}, u32[]{:S(2)}, u32[]{:S(2)}) %collective-permute-start.8) | collective-permute-done | bytes 524320 | tf_op jit(solution)/shard_map/ppermute | solution.py:39
  60.0 0.2 slice_add_fusion
  60.2 1.4 %collective-permute-start.9 = (bf16[128,1024]{1,0:T(8,128)(2,1)S(1)}, bf16[128,1024]{1,0:T(8,128)(2,1)S(1)}, u32[]{:S(2)}, u32[]{:S(2)}) collective-permute-start(bf16[128,1024]{1,0:T(8,128)(2,1)S(1)} %slice.147), channel_id=1, source_target_pairs={{0,16},{4,12},{8,24},{12,4},{16,0},{20,28},{24,8},{28,20},{1,17},{... | collective-permute-start | bytes 786440 | tf_op jit(solution)/shard_map/ppermute | solution.py:39
  61.7 5.0 %collective-permute-done.9 = bf16[128,1024]{1,0:T(8,128)(2,1)S(1)} collective-permute-done((bf16[128,1024]{1,0:T(8,128)(2,1)S(1)}, bf16[128,1024]{1,0:T(8,128)(2,1)S(1)}, u32[]{:S(2)}, u32[]{:S(2)}) %collective-permute-start.9) | collective-permute-done | bytes 262176 | tf_op jit(solution)/shard_map/ppermute | solution.py:39
  66.7 0.1 fusion
  66.7 1.6 %collective-permute-start.10 = (bf16[128,1024]{1,0:T(8,128)(2,1)S(1)}, bf16[128,1024]{1,0:T(8,128)(2,1)S(1)}, u32[]{:S(2)}, u32[]{:S(2)}) collective-permute-start(bf16[128,1024]{1,0:T(8,128)(2,1)S(1)} %fusion), channel_id=1, source_target_pairs={{0,1},{1,0},{2,3},{3,2},{4,6},{5,7},{6,4},{7,5},{8,9},{9,8},{10,11... | collective-permute-start | bytes 786440 | tf_op jit(solution)/shard_map/ppermute | solution.py:47
  68.4 6.5 %collective-permute-done.10 = bf16[128,1024]{1,0:T(8,128)(2,1)S(1)} collective-permute-done((bf16[128,1024]{1,0:T(8,128)(2,1)S(1)}, bf16[128,1024]{1,0:T(8,128)(2,1)S(1)}, u32[]{:S(2)}, u32[]{:S(2)}) %collective-permute-start.10) | collective-permute-done | bytes 262176 | tf_op jit(solution)/shard_map/ppermute | solution.py:47
  74.9 0.1 add_convert_fusion
  74.9 2.7 %collective-permute-start.11 = (bf16[128,1024]{1,0:T(8,128)(2,1)S(1)}, bf16[128,1024]{1,0:T(8,128)(2,1)S(1)}, u32[]{:S(2)}, u32[]{:S(2)}) collective-permute-start(bf16[128,1024]{1,0:T(8,128)(2,1)S(1)} %add_convert_fusion), channel_id=1, source_target_pairs={{0,2},{1,3},{2,0},{3,1},{4,5},{5,4},{6,7},{7,6},{8,10},{9,11},{10,... | collective-permute-start | bytes 786440 | tf_op jit(solution)/shard_map/ppermute | solution.py:47
  77.7 7.5 %collective-permute-done.11 = bf16[128,1024]{1,0:T(8,128)(2,1)S(1)} collective-permute-done((bf16[128,1024]{1,0:T(8,128)(2,1)S(1)}, bf16[128,1024]{1,0:T(8,128)(2,1)S(1)}, u32[]{:S(2)}, u32[]{:S(2)}) %collective-permute-start.11) | collective-permute-done | bytes 262176 | tf_op jit(solution)/shard_map/ppermute | solution.py:47
  85.1 0.9 convert_add_fusion.1
  (24 shorter events, 0.3 us)
Async XLA Ops:
  0.6 12.1 %copy-start.9 = (s32[8]{0:T(128)S(1)}, s32[8]{0:T(128)}, u32[]{:S(2)}) copy-start(s32[8]{0:T(128)} %constant.37.clone) | copy-start | bytes 100
  1.6 19.5 %copy-start = (bf16[1024,1024]{1,0:T(8,128)(2,1)S(1)}, bf16[1024,1024]{1,0:T(8,128)(2,1)}, u32[]{:S(2)}) copy-start(bf16[1024,1024]{1,0:T(8,128)(2,1)} %features_ref.3) | copy-start | bytes 6291460
  1.8 1.5 %collective-permute-start = (bf16[128,512]{1,0:T(8,128)(2,1)S(1)}, bf16[128,512]{1,0:T(8,128)(2,1)S(1)}, u32[]{:S(2)}, u32[]{:S(2)}) collective-permute-start(bf16[128,512]{1,0:T(8,128)(2,1)S(1)} %get-tuple-element.19), channel_id=1, source_target_pairs={{0,4},{4,0},{8,12},{12,8},{16,20},{20,16},{24,28},{28,24},{1,5},{5... | collective-permute-start | bytes 393224 | tf_op jit(solution)/shard_map/ppermute | solution.py:39
  3.3 7.3 %collective-permute-start.1 = (bf16[256,512]{1,0:T(8,128)(2,1)S(1)}, bf16[256,512]{1,0:T(8,128)(2,1)S(1)}, u32[]{:S(2)}, u32[]{:S(2)}) collective-permute-start(bf16[256,512]{1,0:T(8,128)(2,1)S(1)} %pad_maximum_fusion.2), channel_id=1, source_target_pairs={{0,8},{4,20},{8,0},{12,28},{16,24},{20,4},{24,16},{28,12},{1,9},{5... | collective-permute-start | bytes 786440 | tf_op jit(solution)/shard_map/ppermute | solution.py:39
  10.6 9.4 %collective-permute-start.2 = (bf16[512,512]{1,0:T(8,128)(2,1)S(1)}, bf16[512,512]{1,0:T(8,128)(2,1)}, u32[]{:S(2)}, u32[]{:S(2)}) collective-permute-start(bf16[512,512]{1,0:T(8,128)(2,1)S(1)} %pad_maximum_fusion.1), channel_id=1, source_target_pairs={{0,16},{4,12},{8,24},{12,4},{16,0},{20,28},{24,8},{28,20},{1,17},{... | collective-permute-start | bytes 1572872 | tf_op jit(solution)/shard_map/ppermute | solution.py:39
  20.0 6.3 %copy-start.4 = (s32[1024]{0:T(1024)S(1)}, s32[1024]{0:T(1024)}, u32[]{:S(2)}) copy-start(s32[1024]{0:T(1024)} %param.16) | copy-start | bytes 12292
  21.2 5.1 %copy-start.1 = (bf16[1024,1024]{1,0:T(8,128)(2,1)S(1)}, bf16[1024,1024]{1,0:T(8,128)(2,1)}, u32[]{:S(2)}) copy-start(bf16[1024,1024]{1,0:T(8,128)(2,1)} %in_ref.1) | copy-start | bytes 6291460
  21.2 5.1 %copy-start.2 = (bf16[1024,1024]{1,0:T(8,128)(2,1)S(1)}, bf16[1024,1024]{1,0:T(8,128)(2,1)}, u32[]{:S(2)}) copy-start(bf16[1024,1024]{1,0:T(8,128)(2,1)} %out_ref.1) | copy-start | bytes 6291460
  21.2 5.1 %copy-start.3 = (s32[1024]{0:T(1024)S(1)}, s32[1024]{0:T(1024)}, u32[]{:S(2)}) copy-start(s32[1024]{0:T(1024)} %param.15) | copy-start | bytes 12292
  23.6 2.7 %collective-permute-start.3 = (bf16[1024,512]{1,0:T(8,128)(2,1)S(1)}, bf16[1024,512]{1,0:T(8,128)(2,1)S(1)}, u32[]{:S(2)}, u32[]{:S(2)}) collective-permute-start(bf16[1024,512]{1,0:T(8,128)(2,1)S(1)} %queries.1.mine_ref), channel_id=1, source_target_pairs={{0,4},{4,0},{8,12},{12,8},{16,20},{20,16},{24,28},{28,24},{1,5},{5... | collective-permute-start | bytes 3145736 | tf_op jit(solution)/shard_map/ppermute | solution.py:39
  26.3 7.1 %copy-start.7 = (s32[8]{0:T(128)S(1)}, s32[8]{0:T(128)}, u32[]{:S(2)}) copy-start(s32[8]{0:T(128)} %constant.36.clone) | copy-start | bytes 100
  26.3 7.1 %copy-start.8 = (s32[8]{0:T(128)S(1)}, s32[8]{0:T(128)}, u32[]{:S(2)}) copy-start(s32[8]{0:T(128)} %constant.35.clone) | copy-start | bytes 100
  33.3 1.5 %collective-permute-start.4 = (f32[4,1024]{1,0:T(4,128)S(1)}, f32[4,1024]{1,0:T(4,128)S(1)}, u32[]{:S(2)}, u32[]{:S(2)}) collective-permute-start(f32[4,1024]{1,0:T(4,128)S(1)} %get-tuple-element.7), channel_id=1, source_target_pairs={{0,4},{4,0},{8,12},{12,8},{16,20},{20,16},{24,28},{28,24},{1,5},{5... | collective-permute-start | bytes 49160 | tf_op jit(solution)/shard_map/ppermute | solution.py:39
  34.9 4.4 %collective-permute-start.5 = (f32[4,1024]{1,0:T(4,128)S(1)}, f32[4,1024]{1,0:T(4,128)S(1)}, u32[]{:S(2)}, u32[]{:S(2)}) collective-permute-start(f32[4,1024]{1,0:T(4,128)S(1)} %pad_maximum_fusion.3), channel_id=1, source_target_pairs={{0,8},{4,12},{8,0},{12,4},{16,24},{20,28},{24,16},{28,20},{1,9},{5... | collective-permute-start | bytes 49160 | tf_op jit(solution)/shard_map/ppermute | solution.py:39
  39.4 3.9 %collective-permute-start.6 = (f32[4,1024]{1,0:T(4,128)S(1)}, f32[4,1024]{1,0:T(4,128)S(1)}, u32[]{:S(2)}, u32[]{:S(2)}) collective-permute-start(f32[4,1024]{1,0:T(4,128)S(1)} %pad_maximum_fusion.4), channel_id=1, source_target_pairs={{0,16},{4,20},{8,24},{12,28},{16,0},{20,4},{24,8},{28,12},{1,17},{... | collective-permute-start | bytes 49160 | tf_op jit(solution)/shard_map/ppermute | solution.py:39
  41.0 2.4 %copy-start.5 = (s32[1024]{0:T(1024)S(1)}, s32[1024]{0:T(1024)}, u32[]{:S(2)}) copy-start(s32[1024]{0:T(1024)} %param.17) | copy-start | bytes 12292
  43.4 4.3 %copy-start.6 = (f32[1024]{0:T(1024)}, f32[1024]{0:T(1024)S(1)}, u32[]{:S(2)}) copy-start(f32[1024]{0:T(1024)S(1)} %get-tuple-element.13) | copy-start | bytes 12292
  47.7 2.7 %collective-permute-start.7 = (bf16[512,1024]{1,0:T(8,128)(2,1)S(1)}, bf16[512,1024]{1,0:T(8,128)(2,1)S(1)}, u32[]{:S(2)}, u32[]{:S(2)}) collective-permute-start(bf16[512,1024]{1,0:T(8,128)(2,1)S(1)} %get-tuple-element.11), channel_id=1, source_target_pairs={{0,4},{4,0},{8,12},{12,8},{16,20},{20,16},{24,28},{28,24},{1,5},{5... | collective-permute-start | bytes 3145736 | tf_op jit(solution)/shard_map/ppermute | solution.py:39
  50.8 9.2 %collective-permute-start.8 = (bf16[256,1024]{1,0:T(8,128)(2,1)S(1)}, bf16[256,1024]{1,0:T(8,128)(2,1)S(1)}, u32[]{:S(2)}, u32[]{:S(2)}) collective-permute-start(bf16[256,1024]{1,0:T(8,128)(2,1)S(1)} %slice.146), channel_id=1, source_target_pairs={{0,8},{4,20},{8,0},{12,28},{16,24},{20,4},{24,16},{28,12},{1,9},{5... | collective-permute-start | bytes 1572872 | tf_op jit(solution)/shard_map/ppermute | solution.py:39
  60.2 6.4 %collective-permute-start.9 = (bf16[128,1024]{1,0:T(8,128)(2,1)S(1)}, bf16[128,1024]{1,0:T(8,128)(2,1)S(1)}, u32[]{:S(2)}, u32[]{:S(2)}) collective-permute-start(bf16[128,1024]{1,0:T(8,128)(2,1)S(1)} %slice.147), channel_id=1, source_target_pairs={{0,16},{4,12},{8,24},{12,4},{16,0},{20,28},{24,8},{28,20},{1,17},{... | collective-permute-start | bytes 786440 | tf_op jit(solution)/shard_map/ppermute | solution.py:39
  66.7 8.1 %collective-permute-start.10 = (bf16[128,1024]{1,0:T(8,128)(2,1)S(1)}, bf16[128,1024]{1,0:T(8,128)(2,1)S(1)}, u32[]{:S(2)}, u32[]{:S(2)}) collective-permute-start(bf16[128,1024]{1,0:T(8,128)(2,1)S(1)} %fusion), channel_id=1, source_target_pairs={{0,1},{1,0},{2,3},{3,2},{4,6},{5,7},{6,4},{7,5},{8,9},{9,8},{10,11... | collective-permute-start | bytes 786440 | tf_op jit(solution)/shard_map/ppermute | solution.py:47
  74.9 10.2 %collective-permute-start.11 = (bf16[128,1024]{1,0:T(8,128)(2,1)S(1)}, bf16[128,1024]{1,0:T(8,128)(2,1)S(1)}, u32[]{:S(2)}, u32[]{:S(2)}) collective-permute-start(bf16[128,1024]{1,0:T(8,128)(2,1)S(1)} %add_convert_fusion), channel_id=1, source_target_pairs={{0,2},{1,3},{2,0},{3,1},{4,5},{5,4},{6,7},{7,6},{8,10},{9,11},{10,... | collective-permute-start | bytes 786440 | tf_op jit(solution)/shard_map/ppermute | solution.py:47

commit v2 on v1

v2 whole, which is shorter than its diff:
```python
import functools

import jax
import jax.numpy as jnp
from jax import lax
from jax.experimental import pallas as pl
from jax.experimental.pallas import tpu as pltpu
from jax.sharding import PartitionSpec as P


beta = 2.0
BF = jnp.bfloat16
F32 = jnp.float32


def orders(bits):
    turn = len(bits) // 2
    return bits, bits[turn:] + bits[:turn]


def gather_masks(order):
    masks = [0]
    for bit in order:
        masks = masks + [mask ^ (1 << bit) for mask in masks]
    return masks


def scatter_masks(order):
    masks = [0]
    for bit in reversed(order):
        masks = [mask ^ (1 << bit) for mask in masks] + masks
    return masks


def by_core(core, first, second):
    return jnp.where(core == 0, jnp.array(first, jnp.int32), jnp.array(second, jnp.int32))


def cls_swap(value, n, bit_of):
    return lax.ppermute(value, "cls", [(i, i ^ (1 << bit_of[i & 1])) for i in range(n)])


def batch_swap(value, n, depth, bit_of):
    pairs = []
    for i in range(n):
        for j in range(depth):
            pairs.append((i * depth + j, i * depth + (j ^ (1 << bit_of[i & 1]))))
    return lax.ppermute(value, ("cls", "batch"), pairs)


def arrange_kernel(to_ref, from_ref, features_ref, turned_ref, early_ref, late_ref, whole_ref, lined_ref, *, n, rows):
    whole_ref[...] = features_ref[...].T
    for p in range(n):
        start = pl.multiple_of(to_ref[p] * rows, rows)
        turned_ref[p * rows:(p + 1) * rows, :] = whole_ref[pl.ds(start, rows), :]
        start = pl.multiple_of(from_ref[p] * rows, rows)
        lined_ref[p * rows:(p + 1) * rows, :] = whole_ref[pl.ds(start, rows), :]
    split = early_ref.shape[1]
    early_ref[...] = lined_ref[:split, :].T
    late_ref[...] = lined_ref[split:, :].T


def arrange(features, to_place, from_place, n):
    q, f = features.shape
    late = 2 * (f // n)
    vmem = pl.BlockSpec(memory_space=pltpu.VMEM)
    smem = pl.BlockSpec(memory_space=pltpu.SMEM)
    return pl.pallas_call(
        functools.partial(arrange_kernel, n=n, rows=f // n),
        out_shape=(
            jax.ShapeDtypeStruct((f, q), BF),
            jax.ShapeDtypeStruct((q, f - late), BF),
            jax.ShapeDtypeStruct((q, late), BF),
        ),
        in_specs=[smem, smem, vmem],
        out_specs=(vmem, vmem, vmem),
        scratch_shapes=[pltpu.VMEM((f, q), BF), pltpu.VMEM((f, q), BF)],
        compiler_params=pltpu.CompilerParams(vmem_limit_bytes=16 << 20),
        cost_estimate=pl.CostEstimate(flops=0, bytes_accessed=8 * q * f, transcendentals=0),
        name="arrange",
    )(to_place, from_place, features)


def early_kernel(features_ref, *refs, tile):
    *block_refs, out_ref, weight_ref = refs
    rows = block_refs[0].shape[0]
    for p, block_ref in enumerate(block_refs):
        weight_ref[p * rows:(p + 1) * rows, :] = block_ref[...]

    @pl.loop(0, features_ref.shape[0] // tile)
    def _(i):
        part = pl.ds(pl.multiple_of(i * tile, tile), tile)
        out_ref[part, :] = jnp.dot(features_ref[part, :], weight_ref[...], preferred_element_type=F32)


def early_queries(features, blocks):
    q, depth = features.shape
    d = blocks[0].shape[1]
    vmem = pl.BlockSpec(memory_space=pltpu.VMEM)
    return pl.pallas_call(
        functools.partial(early_kernel, tile=256),
        out_shape=jax.ShapeDtypeStruct((q, d), F32),
        in_specs=[vmem] * (1 + len(blocks)),
        out_specs=vmem,
        scratch_shapes=[pltpu.VMEM((depth, d), BF)],
        compiler_params=pltpu.CompilerParams(vmem_limit_bytes=16 << 20),
        cost_estimate=pl.CostEstimate(flops=2 * q * depth * d, bytes_accessed=4 * q * d, transcendentals=0),
        name="early",
    )(features, *blocks)


def to_rows(columns, width):
    r = columns[0].shape[0]
    lane = lax.broadcasted_iota(jnp.int32, (r, width), 1)
    mixed = jnp.broadcast_to(columns[0], (r, width))
    for i, column in enumerate(columns[1:], 1):
        mixed = jnp.where(lane == i, column, mixed)
    return mixed.T[: len(columns), :]


def score_kernel(part_ref, features_ref, mine_ref, other_ref, in_ref, out_ref, in_counts_ref, out_counts_ref,
                 in_weights_ref, out_weights_ref, stats_ref, weight_ref):
    rows = mine_ref.shape[0]

    @pl.when(pl.program_id(0) == 0)
    def _():
        weight_ref[:rows, :] = mine_ref[...]
        weight_ref[rows:, :] = other_ref[...]

    late = jnp.dot(features_ref[...], weight_ref[...], preferred_element_type=F32)
    queries = (part_ref[...] + late).astype(BF) * beta
    stats = []
    for patterns_ref, counts_ref, weights_ref in (
        (in_ref, in_counts_ref, in_weights_ref),
        (out_ref, out_counts_ref, out_weights_ref),
    ):
        scores = lax.dot_general(
            queries, patterns_ref[...], (((1,), (1,)), ((), ())), preferred_element_type=F32
        ) + jnp.log(counts_ref[...].astype(F32))
        top = jnp.max(scores, axis=1, keepdims=True)
        expon = jnp.exp(scores - top)
        weights_ref[...] = expon.astype(BF)
        stats += [top, jnp.sum(expon, axis=1, keepdims=True)]
    stats_ref[...] = to_rows(stats, 128)


def local_weights(part, features, mine, other, inliers, outliers, in_counts, out_counts):
    q, late = features.shape
    d = inliers.shape[1]
    tile = 256
    row = lambda i: (i, 0)
    whole = lambda i: (0, 0)
    ins, outs = inliers.shape[0], outliers.shape[0]
    return pl.pallas_call(
        score_kernel,
        out_shape=(
            jax.ShapeDtypeStruct((q, ins), BF),
            jax.ShapeDtypeStruct((q, outs), BF),
            jax.ShapeDtypeStruct((4, q), F32),
        ),
        grid=(q // tile,),
        in_specs=[
            pl.BlockSpec((tile, d), row),
            pl.BlockSpec((tile, late), row),
            pl.BlockSpec(mine.shape, whole),
            pl.BlockSpec(other.shape, whole),
            pl.BlockSpec((ins, d), whole),
            pl.BlockSpec((outs, d), whole),
            pl.BlockSpec((1, ins), whole),
            pl.BlockSpec((1, outs), whole),
        ],
        out_specs=[
            pl.BlockSpec((tile, ins), row),
            pl.BlockSpec((tile, outs), row),
            pl.BlockSpec((4, tile), lambda i: (0, i)),
        ],
        scratch_shapes=[pltpu.VMEM((late, d), BF)],
        compiler_params=pltpu.CompilerParams(vmem_limit_bytes=32 << 20),
        cost_estimate=pl.CostEstimate(
            flops=2 * q * d * (ins + outs), bytes_accessed=2 * d * (ins + outs), transcendentals=q * (ins + outs)
        ),
        name="scores",
    )(part, features, mine, other, inliers, outliers, in_counts, out_counts)


def merge(mine, other):
    rows = []
    for i in (0, 2):
        top = jnp.maximum(mine[i], other[i])
        rows += [top, mine[i + 1] * jnp.exp(mine[i] - top) + other[i + 1] * jnp.exp(other[i] - top)]
    return jnp.stack(rows)


def outer_kernel(scale_ref, in_ref, out_ref, turned_ref, send_ref, keep_ref, wide_ref):
    q = in_ref.shape[0]
    half = send_ref.shape[0]

    @pl.when(pl.program_id(0) == 0)
    def _():
        for i in range(2):
            wide_ref[i] = jnp.broadcast_to(scale_ref[i:i + 1, :], (128, q)).T

    copies = in_ref.shape[1] // 128
    in_scale = jnp.concatenate([wide_ref[0]] * copies, axis=1)
    out_scale = jnp.concatenate([wide_ref[1]] * copies, axis=1)
    grad = (in_scale * in_ref[...] - out_scale * out_ref[...]).astype(BF)
    send_ref[...] = jnp.dot(turned_ref[:half, :], grad, preferred_element_type=F32).astype(BF)
    keep_ref[...] = jnp.dot(turned_ref[half:, :], grad, preferred_element_type=F32)


def outer(scales, in_sum, out_sum, turned):
    q, d = in_sum.shape
    f = turned.shape[0]
    tile = 256
    column = lambda i: (0, i)
    whole = lambda i: (0, 0)
    return pl.pallas_call(
        outer_kernel,
        out_shape=(jax.ShapeDtypeStruct((f // 2, d), BF), jax.ShapeDtypeStruct((f // 2, d), F32)),
        grid=(d // tile,),
        in_specs=[
            pl.BlockSpec((2, q), whole),
            pl.BlockSpec((q, tile), column),
            pl.BlockSpec((q, tile), column),
            pl.BlockSpec((f, q), whole),
        ],
        out_specs=[pl.BlockSpec((f // 2, tile), column), pl.BlockSpec((f // 2, tile), column)],
        scratch_shapes=[pltpu.VMEM((2, q, 128), F32)],
        compiler_params=pltpu.CompilerParams(vmem_limit_bytes=32 << 20),
        cost_estimate=pl.CostEstimate(flops=2 * q * f * d, bytes_accessed=8 * q * d, transcendentals=0),
        name="outer",
    )(scales, in_sum, out_sum, turned)


def body(features, head_weight, inliers, outliers, inlier_counts, outlier_counts, labels):
    n = lax.axis_size("cls")
    depth = lax.axis_size("batch")
    me = lax.axis_index("cls")
    core = me & 1
    links = list(range(1, n.bit_length() - 1))
    first, second = orders(links)

    held = [head_weight]
    for bit_of in zip(first, second):
        for block in list(held):
            held.append(cls_swap(block, n, bit_of))
    swapped = []
    for block in held:
        swapped.append(cls_swap(block, n, (0, 0)))
    from_first, from_second = gather_masks(first), gather_masks(second)
    mine, other = (
        [masks[:-1] + [mask ^ 1 for mask in others[:-1]] + [masks[-1], others[-1] ^ 1]
         for masks, others in ((from_first, from_second), (from_second, from_first))]
    )
    from_place = me ^ by_core(core, mine, other)
    to_first, to_second = scatter_masks(first), scatter_masks(second)
    to_place = me ^ by_core(core, [m ^ 1 for m in to_second] + to_first, [m ^ 1 for m in to_first] + to_second)
    turned, early_features, late_features = arrange(features, to_place, from_place, n)

    part = early_queries(early_features, held[:-1] + swapped[:-1])
    in_weights, out_weights, stats = local_weights(
        part, late_features, held[-1], swapped[-1], inliers, outliers,
        inlier_counts.reshape(1, -1), outlier_counts.reshape(1, -1),
    )
    whole = stats
    for bit in range(n.bit_length() - 1):
        whole = merge(whole, cls_swap(whole, n, (bit, bit)))
    in_sum = jnp.dot(in_weights, inliers, preferred_element_type=F32)
    out_sum = jnp.dot(out_weights, outliers, preferred_element_type=F32)
    energy = ((whole[0] + jnp.log(whole[1])) - (whole[2] + jnp.log(whole[3]))) / beta
    label_sign = 2.0 * labels.astype(F32) - 1.0
    slope = -label_sign * jax.nn.sigmoid(-label_sign * energy)
    scales = jnp.stack([
        slope * jnp.exp(stats[0] - whole[0]) / whole[1],
        slope * jnp.exp(stats[2] - whole[2]) / whole[3],
    ])
    send, keep = outer(scales, in_sum, out_sum, turned)

    total = keep + cls_swap(send, n, (0, 0)).astype(F32)
    for bit_of in zip(first, second):
        middle = total.shape[0] // 2
        got = cls_swap(total[:middle].astype(BF), n, bit_of)
        total = total[middle:] + got.astype(F32)
    for bit_of in zip(*orders(list(range(depth.bit_length() - 1)))):
        sent = total.astype(BF)
        total = sent.astype(F32) + batch_swap(sent, n, depth, bit_of).astype(F32)
    return energy, total


def solution(mesh):
    placed = (
        P("batch", None),
        P("cls", None),
        P("cls", None),
        P("cls", None),
        P("cls"),
        P("cls"),
        P("batch"),
    )

    return jax.shard_map(body, mesh=mesh, in_specs=placed, out_specs=(P("batch"), P("cls", None)), check_vma=False)
```

time: 86.2 us -> 84.1 us (0.976)
  waiting for transfers between devices: 44.7 us -> 41.4 us
  Pallas kernels: 14.8 us -> 15.9 us
    ppermute x10 -> x13, waiting for transfers between devices: 30.7 us -> 27.4 us  [cls_swap(): lax.ppermute(value, 'cls', [(i, i ^ 1 << bit_of[i & 1]) for i in range(n)])]
    unnamed x20 -> x16, local copies, waits for them, and re-layouts: 0.06 us -> 1.63 us
    concatenate x3 -> x0, other arithmetic: 1.18 us -> none  [the longest x2 1.16 us: body(): blocks = jnp.concatenate([blocks, cls_swap(blocks, n, bit_of)])]
    another operation x1 -> x0, local copies, waits for them, and re-layouts: 0.99 us -> none  [body(): pieces = jnp.stack([head_weight[:, :half], head_weight[:, half:]])]
    ppermute x10 -> x13, starting transfers between devices: 12.4 us -> 12.6 us  [cls_swap(): lax.ppermute(value, 'cls', [(i, i ^ 1 << bit_of[i & 1]) for i in range(n)])]
  transfers between devices with their start and end apart: 12 -> 15, of which waited for: 9 -> 9; matrix products, arithmetic and copies ran while one was open for 5% -> 6% of each run, Pallas kernels for 2% -> 5%
where the time goes in v2:
time: 84.1 us; the launch traced here: 83.9 us
  waiting for transfers between devices  41.4 us (49%)
  starting transfers between devices  17 us (20%)
  Pallas kernels  15.9 us (19%)
  matrix products  4.66 us (6%)
  other arithmetic  2.32 us (3%)
  local copies, waits for them, and re-layouts  1.74 us (2%)
  between operations  0.89 us (1%)
    ppermute x13, waiting for transfers between devices, cls_swap(): lax.ppermute(value, 'cls', [(i, i ^ 1 << bit_of[i & 1]) for i in range(n)])  27.4 us
    ppermute x2, waiting for transfers between devices, batch_swap(): return lax.ppermute(value, ('cls', 'batch'), pairs)  14 us
    ppermute x13, starting transfers between devices, cls_swap(): lax.ppermute(value, 'cls', [(i, i ^ 1 << bit_of[i & 1]) for i in range(n)])  12.6 us
    pallas_call x1, Pallas kernels, local_weights(): pl.pallas_call(score_kernel, out_shape=(jax.ShapeDtypeStruct((q, ins), BF...  7.35 us
    ppermute x2, starting transfers between devices, batch_swap(): return lax.ppermute(value, ('cls', 'batch'), pairs)  4.36 us
    pallas_call x1, Pallas kernels, outer(): pl.pallas_call(outer_kernel, out_shape=(jax.ShapeDtypeStruct((f // 2, d),...  4.35 us
    pallas_call x1, Pallas kernels, early_queries(): pl.pallas_call(functools.partial(early_kernel, tile=256), out_shape=jax.S...  2.4 us
    dot_general x1, matrix products, body(): in_sum = jnp.dot(in_weights, inliers, preferred_element_type=F32)  2.33 us
  transfers between devices with their start and end apart: 15, of which 9 were waited for; matrix products, arithmetic and copies ran while one was open for 6% of the time, Pallas kernels for 5%

profile of v2, /device:TPU:0, one launch (start us, length us, event | category | flops | bytes accessed | tf_op | source)
XLA Modules:
  0.0 83.9 jit_solution(13796741979024763134)
XLA Ops:
  0.6 3.0 %collective-permute-start = (bf16[128,1024]{1,0:T(8,128)(2,1)}, bf16[128,1024]{1,0:T(8,128)(2,1)S(1)}, u32[]{:S(2)}, u32[]{:S(2)}) collective-permute-start(bf16[128,1024]{1,0:T(8,128)(2,1)} %refs_0_.1), channel_id=1, source_target_pairs={{0,8},{4,20},{8,0},{12,28},{16,24},{20,4},{24,16},{28,12},{1,9},{5... | collective-permute-start | bytes 786440 | tf_op jit(solution)/shard_map/ppermute | solution.py:40
  3.7 1.5 %collective-permute-start.1 = (bf16[128,1024]{1,0:T(8,128)(2,1)}, bf16[128,1024]{1,0:T(8,128)(2,1)S(1)}, u32[]{:S(2)}, u32[]{:S(2)}) collective-permute-start(bf16[128,1024]{1,0:T(8,128)(2,1)} %refs_0_.1), channel_id=1, source_target_pairs={{0,16},{4,12},{8,24},{12,4},{16,0},{20,28},{24,8},{28,20},{1,17},{... | collective-permute-start | bytes 786440 | tf_op jit(solution)/shard_map/ppermute | solution.py:40
  5.2 5.4 %collective-permute-done.refs_1_ = bf16[128,1024]{1,0:T(8,128)(2,1)S(1)} collective-permute-done((bf16[128,1024]{1,0:T(8,128)(2,1)}, bf16[128,1024]{1,0:T(8,128)(2,1)S(1)}, u32[]{:S(2)}, u32[]{:S(2)}) %collective-permute-start) | collective-permute-done | bytes 262176 | tf_op jit(solution)/shard_map/ppermute | solution.py:40
  10.6 1.5 %collective-permute-start.5 = (bf16[128,1024]{1,0:T(8,128)(2,1)S(1)}, bf16[128,1024]{1,0:T(8,128)(2,1)S(1)}, u32[]{:S(2)}, u32[]{:S(2)}) collective-permute-start(bf16[128,1024]{1,0:T(8,128)(2,1)S(1)} %collective-permute-done.refs_1_), channel_id=1, source_target_pairs={{0,16},{4,12},{8,24},{12,4},{16,0},{20,28},{24,8},{28,20},{1,17},{... | collective-permute-start | bytes 786440 | tf_op jit(solution)/shard_map/ppermute | solution.py:40
  12.0 0.0 collective-permute-start.2
  12.0 0.0 collective-permute-done.1.refs_2_
  12.0 0.5 collective-permute-start.4
  12.5 0.0 collective-permute-start.3
  12.5 4.4 %collective-permute-done.5.mine_ref = bf16[128,1024]{1,0:T(8,128)(2,1)S(1)} collective-permute-done((bf16[128,1024]{1,0:T(8,128)(2,1)S(1)}, bf16[128,1024]{1,0:T(8,128)(2,1)S(1)}, u32[]{:S(2)}, u32[]{:S(2)}) %collective-permute-start.5) | collective-permute-done | bytes 262176 | tf_op jit(solution)/shard_map/ppermute | solution.py:40
  16.9 0.0 collective-permute-start.6
  16.9 0.7 fusion.1
  17.6 1.6 %copy-done = bf16[1024,1024]{1,0:T(8,128)(2,1)S(1)} copy-done((bf16[1024,1024]{1,0:T(8,128)(2,1)S(1)}, bf16[1024,1024]{1,0:T(8,128)(2,1)}, u32[]{:S(2)}) %copy-start) | copy-done | bytes 2097176
  19.2 1.8 %arrange.1 = (bf16[1024,1024]{1,0:T(8,128)(2,1)S(1)}, bf16[1024,768]{1,0:T(8,128)(2,1)S(1)}, bf16[1024,256]{1,0:T(8,128)(2,1)S(1)}) custom-call(s32[8]{0:T(128)S(1)} %get-tuple-element.48.to_ref, s32[8]{0:T(128)S(1)} %get-tuple-element.49.from_ref, bf16[1024,1024]{1,0:T(8,128)(2,1)S(1)} %copy-done), custom_call_target="tpu_custom_call" | custom-call | bytes 8388608 | tf_op jit(solution)/shard_map/arrange/pallas_call | solution.py:68
  21.1 0.0 collective-permute-done.2.refs_3_
  21.1 0.0 collective-permute-done.4.refs_5_
  21.1 0.0 collective-permute-done.3.refs_4_
  21.1 0.0 copy-start.2
  21.1 0.0 copy-start.3
  21.1 0.0 copy-start.4
  21.1 0.0 copy-start.5
  21.1 2.4 %early.1.part_ref = f32[1024,1024]{1,0:T(8,128)S(1)} custom-call(bf16[1024,768]{1,0:T(8,128)(2,1)S(1)} %get-tuple-element.10.features_ref, bf16[128,1024]{1,0:T(8,128)(2,1)S(1)} %copy-done.1, bf16[128,1024]{1,0:T(8,128)(2,1)S(1)} %collective-permute-done.refs_1_, bf16[128,1024]{1,0:T(8,128)(2,1)S(1)} %collective-permute-done.1.refs_2_, ...), custom_call_target="tpu_custom_call" | custom-call | flops 1610612736 | bytes 4194304 | tf_op jit(solution)/shard_map/early/pallas_call | solution.py:100
  23.5 0.0 collective-permute-done.6.other_ref
  23.6 7.3 %scores.1 = (bf16[1024,1024]{1,0:T(8,128)(2,1)S(1)}, bf16[1024,1024]{1,0:T(8,128)(2,1)S(1)}, f32[4,1024]{1,0:T(4,128)S(1)}) custom-call(f32[1024,1024]{1,0:T(8,128)S(1)} %early.1.part_ref, bf16[1024,256]{1,0:T(8,128)(2,1)S(1)} %get-tuple-element.11.features_ref, bf16[128,1024]{1,0:T(8,128)(2,1)S(1)} %collective-permute-done.5.mine_ref, ...), custom_call_target="tpu_custom_call" | custom-call | flops 4294967296 | bytes 4194304 | tf_op jit(solution)/shard_map/scores/pallas_call | solution.py:154
  30.9 0.6 collective-permute-start.7
  31.5 0.8 collective-permute-done.7
  32.4 2.4 %collective-permute-start.8 = (f32[4,1024]{1,0:T(4,128)S(1)}, f32[4,1024]{1,0:T(4,128)S(1)}, u32[]{:S(2)}, u32[]{:S(2)}) collective-permute-start(f32[4,1024]{1,0:T(4,128)S(1)} %pad_maximum_fusion), channel_id=1, source_target_pairs={{0,8},{4,12},{8,0},{12,4},{16,24},{20,28},{24,16},{28,20},{1,9},{5... | collective-permute-start | bytes 49160 | tf_op jit(solution)/shard_map/ppermute | solution.py:40
  34.9 2.3 %fusion.4.in_ref = f32[1024,1024]{1,0:T(8,128)S(1)} fusion(bf16[1024,1024]{1,0:T(8,128)(2,1)S(1)} %get-tuple-element.13, bf16[1024,1024]{1,0:T(8,128)(2,1)S(1)} %copy-done.2), kind=kOutput, calls=%fused_computation.32 | convolution fusion | flops 2147483648 | bytes 8388608 | tf_op jit(solution)/shard_map/dot_general | solution.py:268
  37.3 0.8 collective-permute-start.9
  38.1 2.3 %fusion.5.out_ref = f32[1024,1024]{1,0:T(8,128)S(1)} fusion(bf16[1024,1024]{1,0:T(8,128)(2,1)S(1)} %get-tuple-element.14, bf16[1024,1024]{1,0:T(8,128)(2,1)S(1)} %copy-done.3), kind=kOutput, calls=%fused_computation.33 | convolution fusion | flops 2147483648 | bytes 8388608 | tf_op jit(solution)/shard_map/dot_general | solution.py:269
  40.4 0.7 collective-permute-done.9
  41.2 0.0 copy-start.7
  41.2 4.3 %outer.1 = (bf16[512,1024]{1,0:T(8,128)(2,1)S(1)}, f32[512,1024]{1,0:T(8,128)S(1)}) custom-call(f32[2,1024]{1,0:T(2,128)S(1)} %pad_maximum_fusion.2.scale_ref, f32[1024,1024]{1,0:T(8,128)S(1)} %fusion.4.in_ref, f32[1024,1024]{1,0:T(8,128)S(1)} %fusion.5.out_ref, bf16[1024,1024]{1,0:T(8,128)(2,1)S(1)} %get-tuple-element.15.turned_ref), custom_call_target="tpu_custom_call" | custom-call | flops 2147483648 | bytes 8388608 | tf_op jit(solution)/shard_map/outer/pallas_call | solution.py:217
  45.6 0.1 collective-permute-start.10
  45.7 2.6 %collective-permute-done.10 = bf16[512,1024]{1,0:T(8,128)(2,1)S(1)} collective-permute-done((bf16[512,1024]{1,0:T(8,128)(2,1)S(1)}, bf16[512,1024]{1,0:T(8,128)(2,1)S(1)}, u32[]{:S(2)}, u32[]{:S(2)}) %collective-permute-start.10) | collective-permute-done | bytes 1048608 | tf_op jit(solution)/shard_map/ppermute | solution.py:40
  48.3 0.3 convert_add_fusion
  48.6 0.1 slice.136
  48.7 1.4 %collective-permute-start.11 = (bf16[256,1024]{1,0:T(8,128)(2,1)S(1)}, bf16[256,1024]{1,0:T(8,128)(2,1)S(1)}, u32[]{:S(2)}, u32[]{:S(2)}) collective-permute-start(bf16[256,1024]{1,0:T(8,128)(2,1)S(1)} %slice.136), channel_id=1, source_target_pairs={{0,8},{4,20},{8,0},{12,28},{16,24},{20,4},{24,16},{28,12},{1,9},{5... | collective-permute-start | bytes 1572872 | tf_op jit(solution)/shard_map/ppermute | solution.py:40
  50.1 7.8 %collective-permute-done.11 = bf16[256,1024]{1,0:T(8,128)(2,1)S(1)} collective-permute-done((bf16[256,1024]{1,0:T(8,128)(2,1)S(1)}, bf16[256,1024]{1,0:T(8,128)(2,1)S(1)}, u32[]{:S(2)}, u32[]{:S(2)}) %collective-permute-start.11) | collective-permute-done | bytes 524320 | tf_op jit(solution)/shard_map/ppermute | solution.py:40
  57.9 0.2 slice_add_fusion
  58.1 0.8 collective-permute-start.12
  58.9 5.7 %collective-permute-done.12 = bf16[128,1024]{1,0:T(8,128)(2,1)S(1)} collective-permute-done((bf16[128,1024]{1,0:T(8,128)(2,1)S(1)}, bf16[128,1024]{1,0:T(8,128)(2,1)S(1)}, u32[]{:S(2)}, u32[]{:S(2)}) %collective-permute-start.12) | collective-permute-done | bytes 262176 | tf_op jit(solution)/shard_map/ppermute | solution.py:40
  64.6 0.1 fusion
  64.6 1.6 %collective-permute-start.13 = (bf16[128,1024]{1,0:T(8,128)(2,1)S(1)}, bf16[128,1024]{1,0:T(8,128)(2,1)S(1)}, u32[]{:S(2)}, u32[]{:S(2)}) collective-permute-start(bf16[128,1024]{1,0:T(8,128)(2,1)S(1)} %fusion), channel_id=1, source_target_pairs={{0,1},{1,0},{2,3},{3,2},{4,6},{5,7},{6,4},{7,5},{8,9},{9,8},{10,11... | collective-permute-start | bytes 786440 | tf_op jit(solution)/shard_map/ppermute | solution.py:48
  66.3 6.5 %collective-permute-done.13 = bf16[128,1024]{1,0:T(8,128)(2,1)S(1)} collective-permute-done((bf16[128,1024]{1,0:T(8,128)(2,1)S(1)}, bf16[128,1024]{1,0:T(8,128)(2,1)S(1)}, u32[]{:S(2)}, u32[]{:S(2)}) %collective-permute-start.13) | collective-permute-done | bytes 262176 | tf_op jit(solution)/shard_map/ppermute | solution.py:48
  72.8 0.1 add_convert_fusion
  72.8 2.7 %collective-permute-start.14 = (bf16[128,1024]{1,0:T(8,128)(2,1)S(1)}, bf16[128,1024]{1,0:T(8,128)(2,1)S(1)}, u32[]{:S(2)}, u32[]{:S(2)}) collective-permute-start(bf16[128,1024]{1,0:T(8,128)(2,1)S(1)} %add_convert_fusion), channel_id=1, source_target_pairs={{0,2},{1,3},{2,0},{3,1},{4,5},{5,4},{6,7},{7,6},{8,10},{9,11},{10,... | collective-permute-start | bytes 786440 | tf_op jit(solution)/shard_map/ppermute | solution.py:48
  75.6 7.5 %collective-permute-done.14 = bf16[128,1024]{1,0:T(8,128)(2,1)S(1)} collective-permute-done((bf16[128,1024]{1,0:T(8,128)(2,1)S(1)}, bf16[128,1024]{1,0:T(8,128)(2,1)S(1)}, u32[]{:S(2)}, u32[]{:S(2)}) %collective-permute-start.14) | collective-permute-done | bytes 262176 | tf_op jit(solution)/shard_map/ppermute | solution.py:48
  83.0 0.9 %convert_add_fusion.1 = f32[128,1024]{1,0:T(8,128)} fusion(bf16[128,1024]{1,0:T(8,128)(2,1)S(1)} %collective-permute-done.14, bf16[128,1024]{1,0:T(8,128)(2,1)S(1)} %add_convert_fusion), kind=kLoop, calls=%fused_computation.6 | loop fusion | flops 393216 | bytes 1048576 | tf_op jit(solution)/shard_map/add | solution.py:286
  (20 shorter events, 0.3 us)
Async XLA Ops:
  0.6 9.9 %collective-permute-start = (bf16[128,1024]{1,0:T(8,128)(2,1)}, bf16[128,1024]{1,0:T(8,128)(2,1)S(1)}, u32[]{:S(2)}, u32[]{:S(2)}) collective-permute-start(bf16[128,1024]{1,0:T(8,128)(2,1)} %refs_0_.1), channel_id=1, source_target_pairs={{0,8},{4,20},{8,0},{12,28},{16,24},{20,4},{24,16},{28,12},{1,9},{5... | collective-permute-start | bytes 786440 | tf_op jit(solution)/shard_map/ppermute | solution.py:40
  3.7 8.4 %collective-permute-start.1 = (bf16[128,1024]{1,0:T(8,128)(2,1)}, bf16[128,1024]{1,0:T(8,128)(2,1)S(1)}, u32[]{:S(2)}, u32[]{:S(2)}) collective-permute-start(bf16[128,1024]{1,0:T(8,128)(2,1)} %refs_0_.1), channel_id=1, source_target_pairs={{0,16},{4,12},{8,24},{12,4},{16,0},{20,28},{24,8},{28,20},{1,17},{... | collective-permute-start | bytes 786440 | tf_op jit(solution)/shard_map/ppermute | solution.py:40
  10.6 6.4 %collective-permute-start.5 = (bf16[128,1024]{1,0:T(8,128)(2,1)S(1)}, bf16[128,1024]{1,0:T(8,128)(2,1)S(1)}, u32[]{:S(2)}, u32[]{:S(2)}) collective-permute-start(bf16[128,1024]{1,0:T(8,128)(2,1)S(1)} %collective-permute-done.refs_1_), channel_id=1, source_target_pairs={{0,16},{4,12},{8,24},{12,4},{16,0},{20,28},{24,8},{28,20},{1,17},{... | collective-permute-start | bytes 786440 | tf_op jit(solution)/shard_map/ppermute | solution.py:40
  12.0 9.0 %collective-permute-start.2 = (bf16[128,1024]{1,0:T(8,128)(2,1)}, bf16[128,1024]{1,0:T(8,128)(2,1)S(1)}, u32[]{:S(2)}, u32[]{:S(2)}) collective-permute-start(bf16[128,1024]{1,0:T(8,128)(2,1)} %refs_0_.1), channel_id=1, source_target_pairs={{0,4},{4,0},{8,12},{12,8},{16,20},{20,16},{24,28},{28,24},{1,5},{5... | collective-permute-start | bytes 786440 | tf_op jit(solution)/shard_map/ppermute | solution.py:40
  12.0 9.0 %collective-permute-start.4 = (bf16[128,1024]{1,0:T(8,128)(2,1)S(1)}, bf16[128,1024]{1,0:T(8,128)(2,1)S(1)}, u32[]{:S(2)}, u32[]{:S(2)}) collective-permute-start(bf16[128,1024]{1,0:T(8,128)(2,1)S(1)} %collective-permute-done.1.refs_2_), channel_id=1, source_target_pairs={{0,4},{4,0},{8,12},{12,8},{16,20},{20,16},{24,28},{28,24},{1,5},{5... | collective-permute-start | bytes 786440 | tf_op jit(solution)/shard_map/ppermute | solution.py:40
  12.5 8.5 %collective-permute-start.3 = (bf16[128,1024]{1,0:T(8,128)(2,1)S(1)}, bf16[128,1024]{1,0:T(8,128)(2,1)S(1)}, u32[]{:S(2)}, u32[]{:S(2)}) collective-permute-start(bf16[128,1024]{1,0:T(8,128)(2,1)S(1)} %collective-permute-done.refs_1_), channel_id=1, source_target_pairs={{0,4},{4,0},{8,12},{12,8},{16,20},{20,16},{24,28},{28,24},{1,5},{5... | collective-permute-start | bytes 786440 | tf_op jit(solution)/shard_map/ppermute | solution.py:40
  16.9 6.6 %collective-permute-start.6 = (bf16[128,1024]{1,0:T(8,128)(2,1)S(1)}, bf16[128,1024]{1,0:T(8,128)(2,1)S(1)}, u32[]{:S(2)}, u32[]{:S(2)}) collective-permute-start(bf16[128,1024]{1,0:T(8,128)(2,1)S(1)} %collective-permute-done.5.mine_ref), channel_id=1, source_target_pairs={{0,4},{4,0},{8,12},{12,8},{16,20},{20,16},{24,28},{28,24},{1,5},{5... | collective-permute-start | bytes 786440 | tf_op jit(solution)/shard_map/ppermute | solution.py:40
  17.6 1.6 %copy-start = (bf16[1024,1024]{1,0:T(8,128)(2,1)S(1)}, bf16[1024,1024]{1,0:T(8,128)(2,1)}, u32[]{:S(2)}) copy-start(bf16[1024,1024]{1,0:T(8,128)(2,1)} %features_ref.1) | copy-start | bytes 6291460
  19.2 1.9 %copy-start.1 = (bf16[128,1024]{1,0:T(8,128)(2,1)S(1)}, bf16[128,1024]{1,0:T(8,128)(2,1)}, u32[]{:S(2)}) copy-start(bf16[128,1024]{1,0:T(8,128)(2,1)} %refs_0_.1) | copy-start | bytes 786436
  21.1 2.5 %copy-start.2 = (bf16[1024,1024]{1,0:T(8,128)(2,1)S(1)}, bf16[1024,1024]{1,0:T(8,128)(2,1)}, u32[]{:S(2)}) copy-start(bf16[1024,1024]{1,0:T(8,128)(2,1)} %in_ref.1) | copy-start | bytes 6291460
  21.1 2.5 %copy-start.3 = (bf16[1024,1024]{1,0:T(8,128)(2,1)S(1)}, bf16[1024,1024]{1,0:T(8,128)(2,1)}, u32[]{:S(2)}) copy-start(bf16[1024,1024]{1,0:T(8,128)(2,1)} %out_ref.1) | copy-start | bytes 6291460
  21.1 2.5 %copy-start.4 = (s32[1024]{0:T(1024)S(1)}, s32[1024]{0:T(1024)}, u32[]{:S(2)}) copy-start(s32[1024]{0:T(1024)} %param.15) | copy-start | bytes 12292
  21.1 2.5 %copy-start.5 = (s32[1024]{0:T(1024)S(1)}, s32[1024]{0:T(1024)}, u32[]{:S(2)}) copy-start(s32[1024]{0:T(1024)} %param.16) | copy-start | bytes 12292
  30.9 1.4 %collective-permute-start.7 = (f32[4,1024]{1,0:T(4,128)S(1)}, f32[4,1024]{1,0:T(4,128)S(1)}, u32[]{:S(2)}, u32[]{:S(2)}) collective-permute-start(f32[4,1024]{1,0:T(4,128)S(1)} %get-tuple-element.12), channel_id=1, source_target_pairs={{0,4},{4,0},{8,12},{12,8},{16,20},{20,16},{24,28},{28,24},{1,5},{5... | collective-permute-start | bytes 49160 | tf_op jit(solution)/shard_map/ppermute | solution.py:40
  32.4 4.8 %collective-permute-start.8 = (f32[4,1024]{1,0:T(4,128)S(1)}, f32[4,1024]{1,0:T(4,128)S(1)}, u32[]{:S(2)}, u32[]{:S(2)}) collective-permute-start(f32[4,1024]{1,0:T(4,128)S(1)} %pad_maximum_fusion), channel_id=1, source_target_pairs={{0,8},{4,12},{8,0},{12,4},{16,24},{20,28},{24,16},{28,20},{1,9},{5... | collective-permute-start | bytes 49160 | tf_op jit(solution)/shard_map/ppermute | solution.py:40
  37.3 3.8 %collective-permute-start.9 = (f32[4,1024]{1,0:T(4,128)S(1)}, f32[4,1024]{1,0:T(4,128)S(1)}, u32[]{:S(2)}, u32[]{:S(2)}) collective-permute-start(f32[4,1024]{1,0:T(4,128)S(1)} %pad_maximum_fusion.1), channel_id=1, source_target_pairs={{0,16},{4,20},{8,24},{12,28},{16,0},{20,4},{24,8},{28,12},{1,17},{... | collective-permute-start | bytes 49160 | tf_op jit(solution)/shard_map/ppermute | solution.py:40
  38.1 3.0 %copy-start.6 = (s32[1024]{0:T(1024)S(1)}, s32[1024]{0:T(1024)}, u32[]{:S(2)}) copy-start(s32[1024]{0:T(1024)} %param.17) | copy-start | bytes 12292
  41.2 4.4 %copy-start.7 = (f32[1024]{0:T(1024)}, f32[1024]{0:T(1024)S(1)}, u32[]{:S(2)}) copy-start(f32[1024]{0:T(1024)S(1)} %get-tuple-element.19) | copy-start | bytes 12292
  45.6 2.7 %collective-permute-start.10 = (bf16[512,1024]{1,0:T(8,128)(2,1)S(1)}, bf16[512,1024]{1,0:T(8,128)(2,1)S(1)}, u32[]{:S(2)}, u32[]{:S(2)}) collective-permute-start(bf16[512,1024]{1,0:T(8,128)(2,1)S(1)} %get-tuple-element.17), channel_id=1, source_target_pairs={{0,4},{4,0},{8,12},{12,8},{16,20},{20,16},{24,28},{28,24},{1,5},{5... | collective-permute-start | bytes 3145736 | tf_op jit(solution)/shard_map/ppermute | solution.py:40
  48.7 9.2 %collective-permute-start.11 = (bf16[256,1024]{1,0:T(8,128)(2,1)S(1)}, bf16[256,1024]{1,0:T(8,128)(2,1)S(1)}, u32[]{:S(2)}, u32[]{:S(2)}) collective-permute-start(bf16[256,1024]{1,0:T(8,128)(2,1)S(1)} %slice.136), channel_id=1, source_target_pairs={{0,8},{4,20},{8,0},{12,28},{16,24},{20,4},{24,16},{28,12},{1,9},{5... | collective-permute-start | bytes 1572872 | tf_op jit(solution)/shard_map/ppermute | solution.py:40
  58.1 6.4 %collective-permute-start.12 = (bf16[128,1024]{1,0:T(8,128)(2,1)S(1)}, bf16[128,1024]{1,0:T(8,128)(2,1)S(1)}, u32[]{:S(2)}, u32[]{:S(2)}) collective-permute-start(bf16[128,1024]{1,0:T(8,128)(2,1)S(1)} %slice.137), channel_id=1, source_target_pairs={{0,16},{4,12},{8,24},{12,4},{16,0},{20,28},{24,8},{28,20},{1,17},{... | collective-permute-start | bytes 786440 | tf_op jit(solution)/shard_map/ppermute | solution.py:40
  64.6 8.1 %collective-permute-start.13 = (bf16[128,1024]{1,0:T(8,128)(2,1)S(1)}, bf16[128,1024]{1,0:T(8,128)(2,1)S(1)}, u32[]{:S(2)}, u32[]{:S(2)}) collective-permute-start(bf16[128,1024]{1,0:T(8,128)(2,1)S(1)} %fusion), channel_id=1, source_target_pairs={{0,1},{1,0},{2,3},{3,2},{4,6},{5,7},{6,4},{7,5},{8,9},{9,8},{10,11... | collective-permute-start | bytes 786440 | tf_op jit(solution)/shard_map/ppermute | solution.py:48
  72.8 10.2 %collective-permute-start.14 = (bf16[128,1024]{1,0:T(8,128)(2,1)S(1)}, bf16[128,1024]{1,0:T(8,128)(2,1)S(1)}, u32[]{:S(2)}, u32[]{:S(2)}) collective-permute-start(bf16[128,1024]{1,0:T(8,128)(2,1)S(1)} %add_convert_fusion), channel_id=1, source_target_pairs={{0,2},{1,3},{2,0},{3,1},{4,5},{5,4},{6,7},{7,6},{8,10},{9,11},{10,... | collective-permute-start | bytes 786440 | tf_op jit(solution)/shard_map/ppermute | solution.py:48

commit v3 on v2

--- a/solution.py
+++ b/solution.py
@@ -11,6 +11,7 @@
 beta = 2.0
 BF = jnp.bfloat16
 F32 = jnp.float32
+PARTS = 2
 
 
 def orders(bits):
@@ -32,8 +33,9 @@
     return masks
 
 
-def by_core(core, first, second):
-    return jnp.where(core == 0, jnp.array(first, jnp.int32), jnp.array(second, jnp.int32))
+def position(me, masks, p):
+    core = me & 1
+    return me ^ (masks[0][p] + core * (masks[1][p] - masks[0][p]))
 
 
 def cls_swap(value, n, bit_of):
@@ -48,37 +50,39 @@
     return lax.ppermute(value, ("cls", "batch"), pairs)
 
 
-def arrange_kernel(to_ref, from_ref, features_ref, turned_ref, early_ref, late_ref, whole_ref, lined_ref, *, n, rows):
+def arrange_kernel(me_ref, features_ref, turned_ref, early_ref, late_ref, whole_ref, lined_ref,
+                   *, to_masks, from_masks, rows):
+    me = me_ref[0]
     whole_ref[...] = features_ref[...].T
-    for p in range(n):
-        start = pl.multiple_of(to_ref[p] * rows, rows)
+    for p in range(len(to_masks[0])):
+        start = pl.multiple_of(position(me, to_masks, p) * rows, rows)
         turned_ref[p * rows:(p + 1) * rows, :] = whole_ref[pl.ds(start, rows), :]
-        start = pl.multiple_of(from_ref[p] * rows, rows)
+        start = pl.multiple_of(position(me, from_masks, p) * rows, rows)
         lined_ref[p * rows:(p + 1) * rows, :] = whole_ref[pl.ds(start, rows), :]
     split = early_ref.shape[1]
     early_ref[...] = lined_ref[:split, :].T
     late_ref[...] = lined_ref[split:, :].T
 
 
-def arrange(features, to_place, from_place, n):
+def arrange(features, me, to_masks, from_masks, n):
     q, f = features.shape
     late = 2 * (f // n)
     vmem = pl.BlockSpec(memory_space=pltpu.VMEM)
     smem = pl.BlockSpec(memory_space=pltpu.SMEM)
     return pl.pallas_call(
-        functools.partial(arrange_kernel, n=n, rows=f // n),
+        functools.partial(arrange_kernel, to_masks=to_masks, from_masks=from_masks, rows=f // n),
         out_shape=(
             jax.ShapeDtypeStruct((f, q), BF),
             jax.ShapeDtypeStruct((q, f - late), BF),
             jax.ShapeDtypeStruct((q, late), BF),
         ),
-        in_specs=[smem, smem, vmem],
+        in_specs=[smem, vmem],
         out_specs=(vmem, vmem, vmem),
         scratch_shapes=[pltpu.VMEM((f, q), BF), pltpu.VMEM((f, q), BF)],
         compiler_params=pltpu.CompilerParams(vmem_limit_bytes=16 << 20),
         cost_estimate=pl.CostEstimate(flops=0, bytes_accessed=8 * q * f, transcendentals=0),
         name="arrange",
-    )(to_place, from_place, features)
+    )(me.reshape(1), features)
 
 
 def early_kernel(features_ref, *refs, tile):
@@ -191,6 +195,29 @@
     return jnp.stack(rows)
 
 
+def weigh_kernel(weights_ref, patterns_ref, out_ref):
+    out_ref[...] = jnp.dot(weights_ref[...], patterns_ref[...], preferred_element_type=F32)
+
+
+def weigh(weights, patterns, part, parts):
+    q, count = weights.shape
+    width = patterns.shape[1] // parts
+    tile = 256
+    return pl.pallas_call(
+        weigh_kernel,
+        out_shape=jax.ShapeDtypeStruct((q, width), F32),
+        grid=(q // tile,),
+        in_specs=[
+            pl.BlockSpec((tile, count), lambda i: (i, 0)),
+            pl.BlockSpec((count, width), lambda i: (0, part)),
+        ],
+        out_specs=pl.BlockSpec((tile, width), lambda i: (i, 0)),
+        compiler_params=pltpu.CompilerParams(vmem_limit_bytes=16 << 20),
+        cost_estimate=pl.CostEstimate(flops=2 * q * count * width, bytes_accessed=4 * q * width, transcendentals=0),
+        name="weigh",
+    )(weights, patterns)
+
+
 def outer_kernel(scale_ref, in_ref, out_ref, turned_ref, send_ref, keep_ref, wide_ref):
     q = in_ref.shape[0]
     half = send_ref.shape[0]
@@ -226,7 +253,7 @@
         ],
         out_specs=[pl.BlockSpec((f // 2, tile), column), pl.BlockSpec((f // 2, tile), column)],
         scratch_shapes=[pltpu.VMEM((2, q, 128), F32)],
-        compiler_params=pltpu.CompilerParams(vmem_limit_bytes=32 << 20),
+        compiler_params=pltpu.CompilerParams(vmem_limit_bytes=24 << 20),
         cost_estimate=pl.CostEstimate(flops=2 * q * f * d, bytes_accessed=8 * q * d, transcendentals=0),
         name="outer",
     )(scales, in_sum, out_sum, turned)
@@ -236,7 +263,6 @@
     n = lax.axis_size("cls")
     depth = lax.axis_size("batch")
     me = lax.axis_index("cls")
-    core = me & 1
     links = list(range(1, n.bit_length() - 1))
     first, second = orders(links)
 
@@ -248,14 +274,13 @@
     for block in held:
         swapped.append(cls_swap(block, n, (0, 0)))
     from_first, from_second = gather_masks(first), gather_masks(second)
-    mine, other = (
-        [masks[:-1] + [mask ^ 1 for mask in others[:-1]] + [masks[-1], others[-1] ^ 1]
-         for masks, others in ((from_first, from_second), (from_second, from_first))]
-    )
-    from_place = me ^ by_core(core, mine, other)
+    from_masks = [
+        masks[:-1] + [mask ^ 1 for mask in others[:-1]] + [masks[-1], others[-1] ^ 1]
+        for masks, others in ((from_first, from_second), (from_second, from_first))
+    ]
     to_first, to_second = scatter_masks(first), scatter_masks(second)
-    to_place = me ^ by_core(core, [m ^ 1 for m in to_second] + to_first, [m ^ 1 for m in to_first] + to_second)
-    turned, early_features, late_features = arrange(features, to_place, from_place, n)
+    to_masks = [[m ^ 1 for m in to_second] + to_first, [m ^ 1 for m in to_first] + to_second]
+    turned, early_features, late_features = arrange(features, me, to_masks, from_masks, n)
 
     part = early_queries(early_features, held[:-1] + swapped[:-1])
     in_weights, out_weights, stats = local_weights(
@@ -264,9 +289,14 @@
     )
     whole = stats
     for bit in range(n.bit_length() - 1):
-        whole = merge(whole, cls_swap(whole, n, (bit, bit)))
-    in_sum = jnp.dot(in_weights, inliers, preferred_element_type=F32)
-    out_sum = jnp.dot(out_weights, outliers, preferred_element_type=F32)
+        got = cls_swap(whole, n, (bit, bit))
+        whole = merge(whole, got)
+    sums = []
+    for k in range(PARTS):
+        pair = []
+        for weights, patterns in ((in_weights, inliers), (out_weights, outliers)):
+            pair.append(weigh(weights, patterns, k, PARTS))
+        sums.append(pair)
     energy = ((whole[0] + jnp.log(whole[1])) - (whole[2] + jnp.log(whole[3]))) / beta
     label_sign = 2.0 * labels.astype(F32) - 1.0
     slope = -label_sign * jax.nn.sigmoid(-label_sign * energy)
@@ -274,17 +304,23 @@
         slope * jnp.exp(stats[0] - whole[0]) / whole[1],
         slope * jnp.exp(stats[2] - whole[2]) / whole[3],
     ])
-    send, keep = outer(scales, in_sum, out_sum, turned)
-
-    total = keep + cls_swap(send, n, (0, 0)).astype(F32)
-    for bit_of in zip(first, second):
-        middle = total.shape[0] // 2
-        got = cls_swap(total[:middle].astype(BF), n, bit_of)
-        total = total[middle:] + got.astype(F32)
-    for bit_of in zip(*orders(list(range(depth.bit_length() - 1)))):
-        sent = total.astype(BF)
-        total = sent.astype(F32) + batch_swap(sent, n, depth, bit_of).astype(F32)
-    return energy, total
+
+    columns = []
+    for in_sum, out_sum in sums:
+        send, keep = outer(scales, in_sum, out_sum, turned)
+        got = cls_swap(send, n, (0, 0))
+        total = keep + got.astype(F32)
+        for bit_of in zip(first, second):
+            middle = total.shape[0] // 2
+            sent = total[:middle].astype(BF)
+            got = cls_swap(sent, n, bit_of)
+            total = total[middle:] + got.astype(F32)
+        for bit_of in zip(*orders(list(range(depth.bit_length() - 1)))):
+            sent = total.astype(BF)
+            got = batch_swap(sent, n, depth, bit_of)
+            total = sent.astype(F32) + got.astype(F32)
+        columns.append(total)
+    return energy, jnp.concatenate(columns, axis=1)
 
 
 def solution(mesh):

time: 84.1 us -> 77.1 us (0.917)
  waiting for transfers between devices: 41.4 us -> 22.7 us
  starting transfers between devices: 17 us -> 26.9 us
  Pallas kernels: 15.9 us -> 22.8 us
  matrix products: 4.66 us -> 0 us
    ppermute x2 -> x4, waiting for transfers between devices: 14 us -> 4.02 us  [batch_swap(): return lax.ppermute(value, ('cls', 'batch'), pairs)]
    ppermute x13 -> x16, waiting for transfers between devices: 27.4 us -> 18.7 us  [cls_swap(): lax.ppermute(value, 'cls', [(i, i ^ 1 << bit_of[i & 1]) for i in range(n)])]
    pallas_call x1 -> x5, Pallas kernels: 1.83 us -> 8.67 us  [the longest x4 7.38 us: weigh(): pl.pallas_call(weigh_kernel, out_shape=jax.ShapeDtypeStruct((q, width), F...]
    ppermute x2 -> x4, starting transfers between devices: 4.36 us -> 10.3 us  [batch_swap(): return lax.ppermute(value, ('cls', 'batch'), pairs)]
    dot_general x2 -> x0, matrix products: 4.66 us -> none  [the longest x1 2.33 us: body(): in_sum = jnp.dot(in_weights, inliers, preferred_element_type=F32)]
    ppermute x13 -> x16, starting transfers between devices: 12.6 us -> 16.6 us  [cls_swap(): lax.ppermute(value, 'cls', [(i, i ^ 1 << bit_of[i & 1]) for i in range(n)])]
    pallas_call x1 -> x2, Pallas kernels: 4.35 us -> 4.59 us  [outer(): pl.pallas_call(outer_kernel, out_shape=(jax.ShapeDtypeStruct((f // 2, d),...]
  transfers between devices with their start and end apart: 15 -> 20, of which waited for: 9 -> 11; matrix products, arithmetic and copies ran while one was open for 6% -> 1% of each run, Pallas kernels for 5% -> 17%
where the time goes in v3:
time: 77.1 us; the launch traced here: 76.9 us
  starting transfers between devices  26.9 us (35%)
  Pallas kernels  22.8 us (30%)
  waiting for transfers between devices  22.7 us (29%)
  local copies, waits for them, and re-layouts  1.75 us (2%)
  other arithmetic  1.67 us (2%)
  between operations  0.98 us (1%)
    ppermute x16, waiting for transfers between devices, cls_swap(): lax.ppermute(value, 'cls', [(i, i ^ 1 << bit_of[i & 1]) for i in range(n)])  18.7 us
    ppermute x16, starting transfers between devices, cls_swap(): lax.ppermute(value, 'cls', [(i, i ^ 1 << bit_of[i & 1]) for i in range(n)])  16.6 us
    ppermute x4, starting transfers between devices, batch_swap(): return lax.ppermute(value, ('cls', 'batch'), pairs)  10.3 us
    pallas_call x4, Pallas kernels, weigh(): pl.pallas_call(weigh_kernel, out_shape=jax.ShapeDtypeStruct((q, width), F...  7.38 us
    pallas_call x1, Pallas kernels, local_weights(): pl.pallas_call(score_kernel, out_shape=(jax.ShapeDtypeStruct((q, ins), BF...  7.19 us
    pallas_call x2, Pallas kernels, outer(): pl.pallas_call(outer_kernel, out_shape=(jax.ShapeDtypeStruct((f // 2, d),...  4.59 us
    ppermute x4, waiting for transfers between devices, batch_swap(): return lax.ppermute(value, ('cls', 'batch'), pairs)  4.02 us
    pallas_call x1, Pallas kernels, early_queries(): pl.pallas_call(functools.partial(early_kernel, tile=256), out_shape=jax.S...  2.39 us
  transfers between devices with their start and end apart: 20, of which 11 were waited for; matrix products, arithmetic and copies ran while one was open for 1% of the time, Pallas kernels for 17%

profile of v3, /device:TPU:0, one launch (start us, length us, event | category | flops | bytes accessed | tf_op | source)
XLA Modules:
  0.0 76.9 jit_solution(666797552453450630)
XLA Ops:
  0.6 3.0 %collective-permute-start = (bf16[128,1024]{1,0:T(8,128)(2,1)}, bf16[128,1024]{1,0:T(8,128)(2,1)S(1)}, u32[]{:S(2)}, u32[]{:S(2)}) collective-permute-start(bf16[128,1024]{1,0:T(8,128)(2,1)} %refs_0_.1), channel_id=1, source_target_pairs={{0,8},{4,20},{8,0},{12,28},{16,24},{20,4},{24,16},{28,12},{1,9},{5... | collective-permute-start | bytes 786440 | tf_op jit(solution)/shard_map/ppermute | solution.py:42
  3.7 1.5 %collective-permute-start.1 = (bf16[128,1024]{1,0:T(8,128)(2,1)}, bf16[128,1024]{1,0:T(8,128)(2,1)S(1)}, u32[]{:S(2)}, u32[]{:S(2)}) collective-permute-start(bf16[128,1024]{1,0:T(8,128)(2,1)} %refs_0_.1), channel_id=1, source_target_pairs={{0,16},{4,12},{8,24},{12,4},{16,0},{20,28},{24,8},{28,20},{1,17},{... | collective-permute-start | bytes 786440 | tf_op jit(solution)/shard_map/ppermute | solution.py:42
  5.2 5.4 %collective-permute-done.refs_1_ = bf16[128,1024]{1,0:T(8,128)(2,1)S(1)} collective-permute-done((bf16[128,1024]{1,0:T(8,128)(2,1)}, bf16[128,1024]{1,0:T(8,128)(2,1)S(1)}, u32[]{:S(2)}, u32[]{:S(2)}) %collective-permute-start) | collective-permute-done | bytes 262176 | tf_op jit(solution)/shard_map/ppermute | solution.py:42
  10.6 1.5 %collective-permute-start.5 = (bf16[128,1024]{1,0:T(8,128)(2,1)S(1)}, bf16[128,1024]{1,0:T(8,128)(2,1)S(1)}, u32[]{:S(2)}, u32[]{:S(2)}) collective-permute-start(bf16[128,1024]{1,0:T(8,128)(2,1)S(1)} %collective-permute-done.refs_1_), channel_id=1, source_target_pairs={{0,16},{4,12},{8,24},{12,4},{16,0},{20,28},{24,8},{28,20},{1,17},{... | collective-permute-start | bytes 786440 | tf_op jit(solution)/shard_map/ppermute | solution.py:42
  12.0 0.5 collective-permute-start.4
  12.5 4.4 %collective-permute-done.5.mine_ref = bf16[128,1024]{1,0:T(8,128)(2,1)S(1)} collective-permute-done((bf16[128,1024]{1,0:T(8,128)(2,1)S(1)}, bf16[128,1024]{1,0:T(8,128)(2,1)S(1)}, u32[]{:S(2)}, u32[]{:S(2)}) %collective-permute-start.5) | collective-permute-done | bytes 262176 | tf_op jit(solution)/shard_map/ppermute | solution.py:42
  16.9 1.6 %copy-done.2 = bf16[1024,1024]{1,0:T(8,128)(2,1)S(1)} copy-done((bf16[1024,1024]{1,0:T(8,128)(2,1)S(1)}, bf16[1024,1024]{1,0:T(8,128)(2,1)}, u32[]{:S(2)}) %copy-start.2) | copy-done | bytes 2097176
  18.5 1.3 %arrange.1 = (bf16[1024,1024]{1,0:T(8,128)(2,1)S(1)}, bf16[1024,768]{1,0:T(8,128)(2,1)S(1)}, bf16[1024,256]{1,0:T(8,128)(2,1)S(1)}) custom-call(s32[1]{0:T(128)} %bitcast.me_ref, bf16[1024,1024]{1,0:T(8,128)(2,1)S(1)} %copy-done.2), custom_call_target="tpu_custom_call" | custom-call | bytes 8388608 | tf_op jit(solution)/shard_map/arrange/pallas_call | solution.py:72
  19.9 0.0 copy-start
  19.9 0.0 copy-start.1
  19.9 0.0 copy-start.4
  19.9 0.0 copy-start.5
  19.9 2.4 %early.1.part_ref = f32[1024,1024]{1,0:T(8,128)S(1)} custom-call(bf16[1024,768]{1,0:T(8,128)(2,1)S(1)} %get-tuple-element.12.features_ref, bf16[128,1024]{1,0:T(8,128)(2,1)S(1)} %copy-done.3, bf16[128,1024]{1,0:T(8,128)(2,1)S(1)} %collective-permute-done.refs_1_, bf16[128,1024]{1,0:T(8,128)(2,1)S(1)} %collective-permute-done.1.refs_2_, ...), custom_call_target="tpu_custom_call" | custom-call | flops 1610612736 | bytes 4194304 | tf_op jit(solution)/shard_map/early/pallas_call | solution.py:104
  22.4 7.2 %scores.1 = (bf16[1024,1024]{1,0:T(8,128)(2,1)S(1)}, bf16[1024,1024]{1,0:T(8,128)(2,1)S(1)}, f32[4,1024]{1,0:T(4,128)S(1)}) custom-call(f32[1024,1024]{1,0:T(8,128)S(1)} %early.1.part_ref, bf16[1024,256]{1,0:T(8,128)(2,1)S(1)} %get-tuple-element.13.features_ref, bf16[128,1024]{1,0:T(8,128)(2,1)S(1)} %collective-permute-done.5.mine_ref, ...), custom_call_target="tpu_custom_call" | custom-call | flops 4294967296 | bytes 4194304 | tf_op jit(solution)/shard_map/scores/pallas_call | solution.py:158
  29.6 0.6 collective-permute-start.7
  30.1 0.8 %collective-permute-done.7 = f32[4,1024]{1,0:T(4,128)S(1)} collective-permute-done((f32[4,1024]{1,0:T(4,128)S(1)}, f32[4,1024]{1,0:T(4,128)S(1)}, u32[]{:S(2)}, u32[]{:S(2)}) %collective-permute-start.7) | collective-permute-done | bytes 16416 | tf_op jit(solution)/shard_map/ppermute | solution.py:42
  31.0 2.4 %collective-permute-start.8 = (f32[4,1024]{1,0:T(4,128)S(1)}, f32[4,1024]{1,0:T(4,128)S(1)}, u32[]{:S(2)}, u32[]{:S(2)}) collective-permute-start(f32[4,1024]{1,0:T(4,128)S(1)} %pad_maximum_fusion.1), channel_id=1, source_target_pairs={{0,8},{4,12},{8,0},{12,4},{16,24},{20,28},{24,16},{28,20},{1,9},{5... | collective-permute-start | bytes 49160 | tf_op jit(solution)/shard_map/ppermute | solution.py:42
  33.5 1.8 %weigh.4.in_ref = f32[1024,512]{1,0:T(8,128)S(1)} custom-call(bf16[1024,1024]{1,0:T(8,128)(2,1)S(1)} %get-tuple-element.15.weights_ref, bf16[1024,1024]{1,0:T(8,128)(2,1)S(1)} %copy-done), custom_call_target="tpu_custom_call" | custom-call | flops 1073741824 | bytes 2097152 | tf_op jit(solution)/shard_map/weigh/pallas_call | solution.py:206
  35.4 1.0 %collective-permute-start.9 = (f32[4,1024]{1,0:T(4,128)S(1)}, f32[4,1024]{1,0:T(4,128)S(1)}, u32[]{:S(2)}, u32[]{:S(2)}) collective-permute-start(f32[4,1024]{1,0:T(4,128)S(1)} %pad_maximum_fusion.2), channel_id=1, source_target_pairs={{0,16},{4,20},{8,24},{12,28},{16,0},{20,4},{24,8},{28,12},{1,17},{... | collective-permute-start | bytes 49160 | tf_op jit(solution)/shard_map/ppermute | solution.py:42
  36.4 1.8 %weigh.5.out_ref = f32[1024,512]{1,0:T(8,128)S(1)} custom-call(bf16[1024,1024]{1,0:T(8,128)(2,1)S(1)} %get-tuple-element.16.weights_ref, bf16[1024,1024]{1,0:T(8,128)(2,1)S(1)} %copy-done.1), custom_call_target="tpu_custom_call" | custom-call | flops 1073741824 | bytes 2097152 | tf_op jit(solution)/shard_map/weigh/pallas_call | solution.py:206
  38.3 0.9 %collective-permute-done.9 = f32[4,1024]{1,0:T(4,128)S(1)} collective-permute-done((f32[4,1024]{1,0:T(4,128)S(1)}, f32[4,1024]{1,0:T(4,128)S(1)}, u32[]{:S(2)}, u32[]{:S(2)}) %collective-permute-start.9) | collective-permute-done | bytes 16416 | tf_op jit(solution)/shard_map/ppermute | solution.py:42
  39.3 0.0 copy-start.7
  39.4 2.3 %outer.2 = (bf16[512,512]{1,0:T(8,128)(2,1)S(1)}, f32[512,512]{1,0:T(8,128)S(1)}) custom-call(f32[2,1024]{1,0:T(2,128)S(1)} %pad_maximum_fusion.3.scale_ref, f32[1024,512]{1,0:T(8,128)S(1)} %weigh.4.in_ref, f32[1024,512]{1,0:T(8,128)S(1)} %weigh.5.out_ref, bf16[1024,1024]{1,0:T(8,128)(2,1)S(1)} %get-tuple-element.17.turned_ref), custom_call_target="tpu_custom_call" | custom-call | flops 1073741824 | bytes 4194304 | tf_op jit(solution)/shard_map/outer/pallas_call | solution.py:244
  41.7 0.1 collective-permute-start.10
  41.7 1.9 %weigh.6.in_ref = f32[1024,512]{1,0:T(8,128)S(1)} custom-call(bf16[1024,1024]{1,0:T(8,128)(2,1)S(1)} %get-tuple-element.15.weights_ref, bf16[1024,1024]{1,0:T(8,128)(2,1)S(1)} %copy-done), custom_call_target="tpu_custom_call" | custom-call | flops 1073741824 | bytes 2097152 | tf_op jit(solution)/shard_map/weigh/pallas_call | solution.py:206
  43.6 1.9 %weigh.7.out_ref = f32[1024,512]{1,0:T(8,128)S(1)} custom-call(bf16[1024,1024]{1,0:T(8,128)(2,1)S(1)} %get-tuple-element.16.weights_ref, bf16[1024,1024]{1,0:T(8,128)(2,1)S(1)} %copy-done.1), custom_call_target="tpu_custom_call" | custom-call | flops 1073741824 | bytes 2097152 | tf_op jit(solution)/shard_map/weigh/pallas_call | solution.py:206
  45.5 2.3 %outer.3 = (bf16[512,512]{1,0:T(8,128)(2,1)S(1)}, f32[512,512]{1,0:T(8,128)S(1)}) custom-call(f32[2,1024]{1,0:T(2,128)S(1)} %pad_maximum_fusion.3.scale_ref, f32[1024,512]{1,0:T(8,128)S(1)} %weigh.6.in_ref, f32[1024,512]{1,0:T(8,128)S(1)} %weigh.7.out_ref, bf16[1024,1024]{1,0:T(8,128)(2,1)S(1)} %get-tuple-element.17.turned_ref), custom_call_target="tpu_custom_call" | custom-call | flops 1073741824 | bytes 4194304 | tf_op jit(solution)/shard_map/outer/pallas_call | solution.py:244
  47.8 0.5 collective-permute-start.15
  48.3 0.2 convert_add_fusion.1
  48.5 1.9 %collective-permute-start.11 = (bf16[256,512]{1,0:T(8,128)(2,1)S(1)}, bf16[256,512]{1,0:T(8,128)(2,1)S(1)}, u32[]{:S(2)}, u32[]{:S(2)}) collective-permute-start(bf16[256,512]{1,0:T(8,128)(2,1)S(1)} %slice.165), channel_id=1, source_target_pairs={{0,8},{4,20},{8,0},{12,28},{16,24},{20,4},{24,16},{28,12},{1,9},{5... | collective-permute-start | bytes 786440 | tf_op jit(solution)/shard_map/ppermute | solution.py:42
  50.5 0.2 convert_add_fusion
  50.7 1.3 %collective-permute-start.16 = (bf16[256,512]{1,0:T(8,128)(2,1)S(1)}, bf16[256,512]{1,0:T(8,128)(2,1)S(1)}, u32[]{:S(2)}, u32[]{:S(2)}) collective-permute-start(bf16[256,512]{1,0:T(8,128)(2,1)S(1)} %slice.164), channel_id=1, source_target_pairs={{0,8},{4,20},{8,0},{12,28},{16,24},{20,4},{24,16},{28,12},{1,9},{5... | collective-permute-start | bytes 786440 | tf_op jit(solution)/shard_map/ppermute | solution.py:42
  52.0 3.0 %collective-permute-done.11 = bf16[256,512]{1,0:T(8,128)(2,1)S(1)} collective-permute-done((bf16[256,512]{1,0:T(8,128)(2,1)S(1)}, bf16[256,512]{1,0:T(8,128)(2,1)S(1)}, u32[]{:S(2)}, u32[]{:S(2)}) %collective-permute-start.11) | collective-permute-done | bytes 262176 | tf_op jit(solution)/shard_map/ppermute | solution.py:42
  55.0 0.1 slice_add_fusion.1
  55.1 1.0 %collective-permute-start.12 = (bf16[128,512]{1,0:T(8,128)(2,1)S(1)}, bf16[128,512]{1,0:T(8,128)(2,1)S(1)}, u32[]{:S(2)}, u32[]{:S(2)}) collective-permute-start(bf16[128,512]{1,0:T(8,128)(2,1)S(1)} %slice.167), channel_id=1, source_target_pairs={{0,16},{4,12},{8,24},{12,4},{16,0},{20,28},{24,8},{28,20},{1,17},{... | collective-permute-start | bytes 393224 | tf_op jit(solution)/shard_map/ppermute | solution.py:42
  56.1 2.4 %collective-permute-done.16 = bf16[256,512]{1,0:T(8,128)(2,1)S(1)} collective-permute-done((bf16[256,512]{1,0:T(8,128)(2,1)S(1)}, bf16[256,512]{1,0:T(8,128)(2,1)S(1)}, u32[]{:S(2)}, u32[]{:S(2)}) %collective-permute-start.16) | collective-permute-done | bytes 262176 | tf_op jit(solution)/shard_map/ppermute | solution.py:42
  58.5 0.1 slice_add_fusion
  58.6 1.2 %collective-permute-start.17 = (bf16[128,512]{1,0:T(8,128)(2,1)S(1)}, bf16[128,512]{1,0:T(8,128)(2,1)S(1)}, u32[]{:S(2)}, u32[]{:S(2)}) collective-permute-start(bf16[128,512]{1,0:T(8,128)(2,1)S(1)} %slice.166), channel_id=1, source_target_pairs={{0,16},{4,12},{8,24},{12,4},{16,0},{20,28},{24,8},{28,20},{1,17},{... | collective-permute-start | bytes 393224 | tf_op jit(solution)/shard_map/ppermute | solution.py:42
  59.8 0.3 collective-permute-done.12
  60.1 2.0 %collective-permute-start.13 = (bf16[128,512]{1,0:T(8,128)(2,1)S(1)}, bf16[128,512]{1,0:T(8,128)(2,1)S(1)}, u32[]{:S(2)}, u32[]{:S(2)}) collective-permute-start(bf16[128,512]{1,0:T(8,128)(2,1)S(1)} %fusion.1), channel_id=1, source_target_pairs={{0,1},{1,0},{2,3},{3,2},{4,6},{5,7},{6,4},{7,5},{8,9},{9,8},{10,11... | collective-permute-start | bytes 393224 | tf_op jit(solution)/shard_map/ppermute | solution.py:50
  62.1 1.5 %collective-permute-done.17 = bf16[128,512]{1,0:T(8,128)(2,1)S(1)} collective-permute-done((bf16[128,512]{1,0:T(8,128)(2,1)S(1)}, bf16[128,512]{1,0:T(8,128)(2,1)S(1)}, u32[]{:S(2)}, u32[]{:S(2)}) %collective-permute-start.17) | collective-permute-done | bytes 131104 | tf_op jit(solution)/shard_map/ppermute | solution.py:42
  63.6 2.2 %collective-permute-start.18 = (bf16[128,512]{1,0:T(8,128)(2,1)S(1)}, bf16[128,512]{1,0:T(8,128)(2,1)S(1)}, u32[]{:S(2)}, u32[]{:S(2)}) collective-permute-start(bf16[128,512]{1,0:T(8,128)(2,1)S(1)} %fusion), channel_id=1, source_target_pairs={{0,1},{1,0},{2,3},{3,2},{4,6},{5,7},{6,4},{7,5},{8,9},{9,8},{10,11... | collective-permute-start | bytes 393224 | tf_op jit(solution)/shard_map/ppermute | solution.py:50
  65.8 0.2 collective-permute-done.13
  66.1 3.0 %collective-permute-start.14 = (bf16[128,512]{1,0:T(8,128)(2,1)S(1)}, bf16[128,512]{1,0:T(8,128)(2,1)S(1)}, u32[]{:S(2)}, u32[]{:S(2)}) collective-permute-start(bf16[128,512]{1,0:T(8,128)(2,1)S(1)} %add_convert_fusion.1), channel_id=1, source_target_pairs={{0,2},{1,3},{2,0},{3,1},{4,5},{5,4},{6,7},{7,6},{8,10},{9,11},{10,... | collective-permute-start | bytes 393224 | tf_op jit(solution)/shard_map/ppermute | solution.py:50
  69.1 0.7 collective-permute-done.18
  69.8 3.1 %collective-permute-start.19 = (bf16[128,512]{1,0:T(8,128)(2,1)S(1)}, bf16[128,512]{1,0:T(8,128)(2,1)S(1)}, u32[]{:S(2)}, u32[]{:S(2)}) collective-permute-start(bf16[128,512]{1,0:T(8,128)(2,1)S(1)} %add_convert_fusion), channel_id=1, source_target_pairs={{0,2},{1,3},{2,0},{3,1},{4,5},{5,4},{6,7},{7,6},{8,10},{9,11},{10,... | collective-permute-start | bytes 393224 | tf_op jit(solution)/shard_map/ppermute | solution.py:50
  72.9 3.1 %collective-permute-done.19 = bf16[128,512]{1,0:T(8,128)(2,1)S(1)} collective-permute-done((bf16[128,512]{1,0:T(8,128)(2,1)S(1)}, bf16[128,512]{1,0:T(8,128)(2,1)S(1)}, u32[]{:S(2)}, u32[]{:S(2)}) %collective-permute-start.19) | collective-permute-done | bytes 131104 | tf_op jit(solution)/shard_map/ppermute | solution.py:50
  76.1 0.8 %pad_maximum_fusion = f32[128,1024]{1,0:T(8,128)} fusion(f32[128,512]{1,0:T(8,128)S(1)} %convert_add_fusion.2, f32[128,512]{1,0:T(8,128)S(1)} %convert_add_fusion.3), kind=kLoop, calls=%fused_computation.6 | loop fusion | flops 131072 | bytes 1048576 | tf_op jit(solution)/shard_map/concatenate | solution.py:323
  (40 shorter events, 0.6 us)
Async XLA Ops:
  0.6 9.9 %collective-permute-start = (bf16[128,1024]{1,0:T(8,128)(2,1)}, bf16[128,1024]{1,0:T(8,128)(2,1)S(1)}, u32[]{:S(2)}, u32[]{:S(2)}) collective-permute-start(bf16[128,1024]{1,0:T(8,128)(2,1)} %refs_0_.1), channel_id=1, source_target_pairs={{0,8},{4,20},{8,0},{12,28},{16,24},{20,4},{24,16},{28,12},{1,9},{5... | collective-permute-start | bytes 786440 | tf_op jit(solution)/shard_map/ppermute | solution.py:42
  3.7 8.4 %collective-permute-start.1 = (bf16[128,1024]{1,0:T(8,128)(2,1)}, bf16[128,1024]{1,0:T(8,128)(2,1)S(1)}, u32[]{:S(2)}, u32[]{:S(2)}) collective-permute-start(bf16[128,1024]{1,0:T(8,128)(2,1)} %refs_0_.1), channel_id=1, source_target_pairs={{0,16},{4,12},{8,24},{12,4},{16,0},{20,28},{24,8},{28,20},{1,17},{... | collective-permute-start | bytes 786440 | tf_op jit(solution)/shard_map/ppermute | solution.py:42
  10.6 6.4 %collective-permute-start.5 = (bf16[128,1024]{1,0:T(8,128)(2,1)S(1)}, bf16[128,1024]{1,0:T(8,128)(2,1)S(1)}, u32[]{:S(2)}, u32[]{:S(2)}) collective-permute-start(bf16[128,1024]{1,0:T(8,128)(2,1)S(1)} %collective-permute-done.refs_1_), channel_id=1, source_target_pairs={{0,16},{4,12},{8,24},{12,4},{16,0},{20,28},{24,8},{28,20},{1,17},{... | collective-permute-start | bytes 786440 | tf_op jit(solution)/shard_map/ppermute | solution.py:42
  12.0 7.8 %collective-permute-start.2 = (bf16[128,1024]{1,0:T(8,128)(2,1)}, bf16[128,1024]{1,0:T(8,128)(2,1)S(1)}, u32[]{:S(2)}, u32[]{:S(2)}) collective-permute-start(bf16[128,1024]{1,0:T(8,128)(2,1)} %refs_0_.1), channel_id=1, source_target_pairs={{0,4},{4,0},{8,12},{12,8},{16,20},{20,16},{24,28},{28,24},{1,5},{5... | collective-permute-start | bytes 786440 | tf_op jit(solution)/shard_map/ppermute | solution.py:42
  12.0 7.8 %collective-permute-start.4 = (bf16[128,1024]{1,0:T(8,128)(2,1)S(1)}, bf16[128,1024]{1,0:T(8,128)(2,1)S(1)}, u32[]{:S(2)}, u32[]{:S(2)}) collective-permute-start(bf16[128,1024]{1,0:T(8,128)(2,1)S(1)} %collective-permute-done.1.refs_2_), channel_id=1, source_target_pairs={{0,4},{4,0},{8,12},{12,8},{16,20},{20,16},{24,28},{28,24},{1,5},{5... | collective-permute-start | bytes 786440 | tf_op jit(solution)/shard_map/ppermute | solution.py:42
  12.5 7.3 %collective-permute-start.3 = (bf16[128,1024]{1,0:T(8,128)(2,1)S(1)}, bf16[128,1024]{1,0:T(8,128)(2,1)S(1)}, u32[]{:S(2)}, u32[]{:S(2)}) collective-permute-start(bf16[128,1024]{1,0:T(8,128)(2,1)S(1)} %collective-permute-done.refs_1_), channel_id=1, source_target_pairs={{0,4},{4,0},{8,12},{12,8},{16,20},{20,16},{24,28},{28,24},{1,5},{5... | collective-permute-start | bytes 786440 | tf_op jit(solution)/shard_map/ppermute | solution.py:42
  16.9 5.4 %collective-permute-start.6 = (bf16[128,1024]{1,0:T(8,128)(2,1)S(1)}, bf16[128,1024]{1,0:T(8,128)(2,1)S(1)}, u32[]{:S(2)}, u32[]{:S(2)}) collective-permute-start(bf16[128,1024]{1,0:T(8,128)(2,1)S(1)} %collective-permute-done.5.mine_ref), channel_id=1, source_target_pairs={{0,4},{4,0},{8,12},{12,8},{16,20},{20,16},{24,28},{28,24},{1,5},{5... | collective-permute-start | bytes 786440 | tf_op jit(solution)/shard_map/ppermute | solution.py:42
  16.9 1.6 %copy-start.2 = (bf16[1024,1024]{1,0:T(8,128)(2,1)S(1)}, bf16[1024,1024]{1,0:T(8,128)(2,1)}, u32[]{:S(2)}) copy-start(bf16[1024,1024]{1,0:T(8,128)(2,1)} %features_ref.1) | copy-start | bytes 6291460
  18.5 1.3 %copy-start.3 = (bf16[128,1024]{1,0:T(8,128)(2,1)S(1)}, bf16[128,1024]{1,0:T(8,128)(2,1)}, u32[]{:S(2)}) copy-start(bf16[128,1024]{1,0:T(8,128)(2,1)} %refs_0_.1) | copy-start | bytes 786436
  19.9 2.5 %copy-start = (bf16[1024,1024]{1,0:T(8,128)(2,1)S(1)}, bf16[1024,1024]{1,0:T(8,128)(2,1)}, u32[]{:S(2)}) copy-start(bf16[1024,1024]{1,0:T(8,128)(2,1)} %patterns_ref.6) | copy-start | bytes 6291460
  19.9 2.5 %copy-start.1 = (bf16[1024,1024]{1,0:T(8,128)(2,1)S(1)}, bf16[1024,1024]{1,0:T(8,128)(2,1)}, u32[]{:S(2)}) copy-start(bf16[1024,1024]{1,0:T(8,128)(2,1)} %patterns_ref.7) | copy-start | bytes 6291460
  19.9 2.5 %copy-start.4 = (s32[1024]{0:T(1024)S(1)}, s32[1024]{0:T(1024)}, u32[]{:S(2)}) copy-start(s32[1024]{0:T(1024)} %param.11) | copy-start | bytes 12292
  19.9 2.5 %copy-start.5 = (s32[1024]{0:T(1024)S(1)}, s32[1024]{0:T(1024)}, u32[]{:S(2)}) copy-start(s32[1024]{0:T(1024)} %param.12) | copy-start | bytes 12292
  29.6 1.4 %collective-permute-start.7 = (f32[4,1024]{1,0:T(4,128)S(1)}, f32[4,1024]{1,0:T(4,128)S(1)}, u32[]{:S(2)}, u32[]{:S(2)}) collective-permute-start(f32[4,1024]{1,0:T(4,128)S(1)} %get-tuple-element.14), channel_id=1, source_target_pairs={{0,4},{4,0},{8,12},{12,8},{16,20},{20,16},{24,28},{28,24},{1,5},{5... | collective-permute-start | bytes 49160 | tf_op jit(solution)/shard_map/ppermute | solution.py:42
  31.0 4.3 %collective-permute-start.8 = (f32[4,1024]{1,0:T(4,128)S(1)}, f32[4,1024]{1,0:T(4,128)S(1)}, u32[]{:S(2)}, u32[]{:S(2)}) collective-permute-start(f32[4,1024]{1,0:T(4,128)S(1)} %pad_maximum_fusion.1), channel_id=1, source_target_pairs={{0,8},{4,12},{8,0},{12,4},{16,24},{20,28},{24,16},{28,20},{1,9},{5... | collective-permute-start | bytes 49160 | tf_op jit(solution)/shard_map/ppermute | solution.py:42
  35.4 3.8 %collective-permute-start.9 = (f32[4,1024]{1,0:T(4,128)S(1)}, f32[4,1024]{1,0:T(4,128)S(1)}, u32[]{:S(2)}, u32[]{:S(2)}) collective-permute-start(f32[4,1024]{1,0:T(4,128)S(1)} %pad_maximum_fusion.2), channel_id=1, source_target_pairs={{0,16},{4,20},{8,24},{12,28},{16,0},{20,4},{24,8},{28,12},{1,17},{... | collective-permute-start | bytes 49160 | tf_op jit(solution)/shard_map/ppermute | solution.py:42
  36.4 2.8 %copy-start.6 = (s32[1024]{0:T(1024)S(1)}, s32[1024]{0:T(1024)}, u32[]{:S(2)}) copy-start(s32[1024]{0:T(1024)} %param.13) | copy-start | bytes 12292
  39.3 2.4 %copy-start.7 = (f32[1024]{0:T(1024)}, f32[1024]{0:T(1024)S(1)}, u32[]{:S(2)}) copy-start(f32[1024]{0:T(1024)S(1)} %get-tuple-element.23) | copy-start | bytes 12292
  41.7 6.6 %collective-permute-start.10 = (bf16[512,512]{1,0:T(8,128)(2,1)S(1)}, bf16[512,512]{1,0:T(8,128)(2,1)S(1)}, u32[]{:S(2)}, u32[]{:S(2)}) collective-permute-start(bf16[512,512]{1,0:T(8,128)(2,1)S(1)} %get-tuple-element.19), channel_id=1, source_target_pairs={{0,4},{4,0},{8,12},{12,8},{16,20},{20,16},{24,28},{28,24},{1,5},{5... | collective-permute-start | bytes 1572872 | tf_op jit(solution)/shard_map/ppermute | solution.py:42
  47.8 2.7 %collective-permute-start.15 = (bf16[512,512]{1,0:T(8,128)(2,1)S(1)}, bf16[512,512]{1,0:T(8,128)(2,1)S(1)}, u32[]{:S(2)}, u32[]{:S(2)}) collective-permute-start(bf16[512,512]{1,0:T(8,128)(2,1)S(1)} %get-tuple-element.21), channel_id=1, source_target_pairs={{0,4},{4,0},{8,12},{12,8},{16,20},{20,16},{24,28},{28,24},{1,5},{5... | collective-permute-start | bytes 1572872 | tf_op jit(solution)/shard_map/ppermute | solution.py:42
  48.5 6.4 %collective-permute-start.11 = (bf16[256,512]{1,0:T(8,128)(2,1)S(1)}, bf16[256,512]{1,0:T(8,128)(2,1)S(1)}, u32[]{:S(2)}, u32[]{:S(2)}) collective-permute-start(bf16[256,512]{1,0:T(8,128)(2,1)S(1)} %slice.165), channel_id=1, source_target_pairs={{0,8},{4,20},{8,0},{12,28},{16,24},{20,4},{24,16},{28,12},{1,9},{5... | collective-permute-start | bytes 786440 | tf_op jit(solution)/shard_map/ppermute | solution.py:42
  50.7 7.8 %collective-permute-start.16 = (bf16[256,512]{1,0:T(8,128)(2,1)S(1)}, bf16[256,512]{1,0:T(8,128)(2,1)S(1)}, u32[]{:S(2)}, u32[]{:S(2)}) collective-permute-start(bf16[256,512]{1,0:T(8,128)(2,1)S(1)} %slice.164), channel_id=1, source_target_pairs={{0,8},{4,20},{8,0},{12,28},{16,24},{20,4},{24,16},{28,12},{1,9},{5... | collective-permute-start | bytes 786440 | tf_op jit(solution)/shard_map/ppermute | solution.py:42
  55.1 5.0 %collective-permute-start.12 = (bf16[128,512]{1,0:T(8,128)(2,1)S(1)}, bf16[128,512]{1,0:T(8,128)(2,1)S(1)}, u32[]{:S(2)}, u32[]{:S(2)}) collective-permute-start(bf16[128,512]{1,0:T(8,128)(2,1)S(1)} %slice.167), channel_id=1, source_target_pairs={{0,16},{4,12},{8,24},{12,4},{16,0},{20,28},{24,8},{28,20},{1,17},{... | collective-permute-start | bytes 393224 | tf_op jit(solution)/shard_map/ppermute | solution.py:42
  58.6 5.0 %collective-permute-start.17 = (bf16[128,512]{1,0:T(8,128)(2,1)S(1)}, bf16[128,512]{1,0:T(8,128)(2,1)S(1)}, u32[]{:S(2)}, u32[]{:S(2)}) collective-permute-start(bf16[128,512]{1,0:T(8,128)(2,1)S(1)} %slice.166), channel_id=1, source_target_pairs={{0,16},{4,12},{8,24},{12,4},{16,0},{20,28},{24,8},{28,20},{1,17},{... | collective-permute-start | bytes 393224 | tf_op jit(solution)/shard_map/ppermute | solution.py:42
  60.1 5.9 %collective-permute-start.13 = (bf16[128,512]{1,0:T(8,128)(2,1)S(1)}, bf16[128,512]{1,0:T(8,128)(2,1)S(1)}, u32[]{:S(2)}, u32[]{:S(2)}) collective-permute-start(bf16[128,512]{1,0:T(8,128)(2,1)S(1)} %fusion.1), channel_id=1, source_target_pairs={{0,1},{1,0},{2,3},{3,2},{4,6},{5,7},{6,4},{7,5},{8,9},{9,8},{10,11... | collective-permute-start | bytes 393224 | tf_op jit(solution)/shard_map/ppermute | solution.py:50
  63.6 6.1 %collective-permute-start.18 = (bf16[128,512]{1,0:T(8,128)(2,1)S(1)}, bf16[128,512]{1,0:T(8,128)(2,1)S(1)}, u32[]{:S(2)}, u32[]{:S(2)}) collective-permute-start(bf16[128,512]{1,0:T(8,128)(2,1)S(1)} %fusion), channel_id=1, source_target_pairs={{0,1},{1,0},{2,3},{3,2},{4,6},{5,7},{6,4},{7,5},{8,9},{9,8},{10,11... | collective-permute-start | bytes 393224 | tf_op jit(solution)/shard_map/ppermute | solution.py:50
  66.1 6.8 %collective-permute-start.14 = (bf16[128,512]{1,0:T(8,128)(2,1)S(1)}, bf16[128,512]{1,0:T(8,128)(2,1)S(1)}, u32[]{:S(2)}, u32[]{:S(2)}) collective-permute-start(bf16[128,512]{1,0:T(8,128)(2,1)S(1)} %add_convert_fusion.1), channel_id=1, source_target_pairs={{0,2},{1,3},{2,0},{3,1},{4,5},{5,4},{6,7},{7,6},{8,10},{9,11},{10,... | collective-permute-start | bytes 393224 | tf_op jit(solution)/shard_map/ppermute | solution.py:50
  69.8 6.2 %collective-permute-start.19 = (bf16[128,512]{1,0:T(8,128)(2,1)S(1)}, bf16[128,512]{1,0:T(8,128)(2,1)S(1)}, u32[]{:S(2)}, u32[]{:S(2)}) collective-permute-start(bf16[128,512]{1,0:T(8,128)(2,1)S(1)} %add_convert_fusion), channel_id=1, source_target_pairs={{0,2},{1,3},{2,0},{3,1},{4,5},{5,4},{6,7},{7,6},{8,10},{9,11},{10,... | collective-permute-start | bytes 393224 | tf_op jit(solution)/shard_map/ppermute | solution.py:50

commit v4 on v3

--- a/solution.py
+++ b/solution.py
@@ -1,4 +1,5 @@
 import functools
+import math
 
 import jax
 import jax.numpy as jnp
@@ -66,7 +67,7 @@
 
 def arrange(features, me, to_masks, from_masks, n):
     q, f = features.shape
-    late = 2 * (f // n)
+    late = f // 2
     vmem = pl.BlockSpec(memory_space=pltpu.VMEM)
     smem = pl.BlockSpec(memory_space=pltpu.SMEM)
     return pl.pallas_call(
@@ -85,16 +86,16 @@
     )(me.reshape(1), features)
 
 
-def early_kernel(features_ref, *refs, tile):
-    *block_refs, out_ref, weight_ref = refs
+def join(block_refs, weight_ref):
     rows = block_refs[0].shape[0]
     for p, block_ref in enumerate(block_refs):
         weight_ref[p * rows:(p + 1) * rows, :] = block_ref[...]
 
-    @pl.loop(0, features_ref.shape[0] // tile)
-    def _(i):
-        part = pl.ds(pl.multiple_of(i * tile, tile), tile)
-        out_ref[part, :] = jnp.dot(features_ref[part, :], weight_ref[...], preferred_element_type=F32)
+
+def early_kernel(features_ref, *refs):
+    *block_refs, out_ref, weight_ref = refs
+    join(block_refs, weight_ref)
+    out_ref[...] = jnp.dot(features_ref[...], weight_ref[...], preferred_element_type=F32)
 
 
 def early_queries(features, blocks):
@@ -102,7 +103,7 @@
     d = blocks[0].shape[1]
     vmem = pl.BlockSpec(memory_space=pltpu.VMEM)
     return pl.pallas_call(
-        functools.partial(early_kernel, tile=256),
+        early_kernel,
         out_shape=jax.ShapeDtypeStruct((q, d), F32),
         in_specs=[vmem] * (1 + len(blocks)),
         out_specs=vmem,
@@ -122,14 +123,12 @@
     return mixed.T[: len(columns), :]
 
 
-def score_kernel(part_ref, features_ref, mine_ref, other_ref, in_ref, out_ref, in_counts_ref, out_counts_ref,
-                 in_weights_ref, out_weights_ref, stats_ref, weight_ref):
-    rows = mine_ref.shape[0]
+def score_kernel(part_ref, features_ref, in_ref, out_ref, in_counts_ref, out_counts_ref, *refs):
+    *block_refs, in_weights_ref, out_weights_ref, stats_ref, weight_ref = refs
 
     @pl.when(pl.program_id(0) == 0)
     def _():
-        weight_ref[:rows, :] = mine_ref[...]
-        weight_ref[rows:, :] = other_ref[...]
+        join(block_refs, weight_ref)
 
     late = jnp.dot(features_ref[...], weight_ref[...], preferred_element_type=F32)
     queries = (part_ref[...] + late).astype(BF) * beta
@@ -148,10 +147,10 @@
     stats_ref[...] = to_rows(stats, 128)
 
 
-def local_weights(part, features, mine, other, inliers, outliers, in_counts, out_counts):
+def local_weights(part, features, blocks, inliers, outliers, in_counts, out_counts):
     q, late = features.shape
     d = inliers.shape[1]
-    tile = 256
+    tile = math.gcd(q, 512)
     row = lambda i: (i, 0)
     whole = lambda i: (0, 0)
     ins, outs = inliers.shape[0], outliers.shape[0]
@@ -166,13 +165,11 @@
         in_specs=[
             pl.BlockSpec((tile, d), row),
             pl.BlockSpec((tile, late), row),
-            pl.BlockSpec(mine.shape, whole),
-            pl.BlockSpec(other.shape, whole),
             pl.BlockSpec((ins, d), whole),
             pl.BlockSpec((outs, d), whole),
             pl.BlockSpec((1, ins), whole),
             pl.BlockSpec((1, outs), whole),
-        ],
+        ] + [pl.BlockSpec(block.shape, whole) for block in blocks],
         out_specs=[
             pl.BlockSpec((tile, ins), row),
             pl.BlockSpec((tile, outs), row),
@@ -184,7 +181,7 @@
             flops=2 * q * d * (ins + outs), bytes_accessed=2 * d * (ins + outs), transcendentals=q * (ins + outs)
         ),
         name="scores",
-    )(part, features, mine, other, inliers, outliers, in_counts, out_counts)
+    )(part, features, inliers, outliers, in_counts, out_counts, *blocks)
 
 
 def merge(mine, other):
@@ -202,59 +199,45 @@
 def weigh(weights, patterns, part, parts):
     q, count = weights.shape
     width = patterns.shape[1] // parts
-    tile = 256
     return pl.pallas_call(
         weigh_kernel,
         out_shape=jax.ShapeDtypeStruct((q, width), F32),
-        grid=(q // tile,),
+        grid=(1,),
         in_specs=[
-            pl.BlockSpec((tile, count), lambda i: (i, 0)),
+            pl.BlockSpec((q, count), lambda i: (0, 0)),
             pl.BlockSpec((count, width), lambda i: (0, part)),
         ],
-        out_specs=pl.BlockSpec((tile, width), lambda i: (i, 0)),
+        out_specs=pl.BlockSpec((q, width), lambda i: (0, 0)),
         compiler_params=pltpu.CompilerParams(vmem_limit_bytes=16 << 20),
         cost_estimate=pl.CostEstimate(flops=2 * q * count * width, bytes_accessed=4 * q * width, transcendentals=0),
         name="weigh",
     )(weights, patterns)
 
 
-def outer_kernel(scale_ref, in_ref, out_ref, turned_ref, send_ref, keep_ref, wide_ref):
-    q = in_ref.shape[0]
+def outer_kernel(scale_ref, in_ref, out_ref, turned_ref, send_ref, keep_ref):
+    q, width = in_ref.shape
     half = send_ref.shape[0]
-
-    @pl.when(pl.program_id(0) == 0)
-    def _():
-        for i in range(2):
-            wide_ref[i] = jnp.broadcast_to(scale_ref[i:i + 1, :], (128, q)).T
-
-    copies = in_ref.shape[1] // 128
-    in_scale = jnp.concatenate([wide_ref[0]] * copies, axis=1)
-    out_scale = jnp.concatenate([wide_ref[1]] * copies, axis=1)
-    grad = (in_scale * in_ref[...] - out_scale * out_ref[...]).astype(BF)
+    copies = width // 128
+
+    def wide(i):
+        return jnp.concatenate([jnp.broadcast_to(scale_ref[i:i + 1, :], (128, q)).T] * copies, axis=1)
+
+    grad = (wide(0) * in_ref[...] - wide(1) * out_ref[...]).astype(BF)
     send_ref[...] = jnp.dot(turned_ref[:half, :], grad, preferred_element_type=F32).astype(BF)
     keep_ref[...] = jnp.dot(turned_ref[half:, :], grad, preferred_element_type=F32)
 
 
 def outer(scales, in_sum, out_sum, turned):
-    q, d = in_sum.shape
+    q, width = in_sum.shape
     f = turned.shape[0]
-    tile = 256
-    column = lambda i: (0, i)
-    whole = lambda i: (0, 0)
+    vmem = pl.BlockSpec(memory_space=pltpu.VMEM)
     return pl.pallas_call(
         outer_kernel,
-        out_shape=(jax.ShapeDtypeStruct((f // 2, d), BF), jax.ShapeDtypeStruct((f // 2, d), F32)),
-        grid=(d // tile,),
-        in_specs=[
-            pl.BlockSpec((2, q), whole),
-            pl.BlockSpec((q, tile), column),
-            pl.BlockSpec((q, tile), column),
-            pl.BlockSpec((f, q), whole),
-        ],
-        out_specs=[pl.BlockSpec((f // 2, tile), column), pl.BlockSpec((f // 2, tile), column)],
-        scratch_shapes=[pltpu.VMEM((2, q, 128), F32)],
-        compiler_params=pltpu.CompilerParams(vmem_limit_bytes=24 << 20),
-        cost_estimate=pl.CostEstimate(flops=2 * q * f * d, bytes_accessed=8 * q * d, transcendentals=0),
+        out_shape=(jax.ShapeDtypeStruct((f // 2, width), BF), jax.ShapeDtypeStruct((f // 2, width), F32)),
+        in_specs=[vmem] * 4,
+        out_specs=(vmem, vmem),
+        compiler_params=pltpu.CompilerParams(vmem_limit_bytes=16 << 20),
+        cost_estimate=pl.CostEstimate(flops=2 * q * f * width, bytes_accessed=8 * q * width, transcendentals=0),
         name="outer",
     )(scales, in_sum, out_sum, turned)
 
@@ -274,17 +257,18 @@
     for block in held:
         swapped.append(cls_swap(block, n, (0, 0)))
     from_first, from_second = gather_masks(first), gather_masks(second)
+    early = n // 4
     from_masks = [
-        masks[:-1] + [mask ^ 1 for mask in others[:-1]] + [masks[-1], others[-1] ^ 1]
+        masks[:early] + [mask ^ 1 for mask in others[:early]] + masks[early:] + [mask ^ 1 for mask in others[early:]]
         for masks, others in ((from_first, from_second), (from_second, from_first))
     ]
     to_first, to_second = scatter_masks(first), scatter_masks(second)
     to_masks = [[m ^ 1 for m in to_second] + to_first, [m ^ 1 for m in to_first] + to_second]
     turned, early_features, late_features = arrange(features, me, to_masks, from_masks, n)
 
-    part = early_queries(early_features, held[:-1] + swapped[:-1])
+    part = early_queries(early_features, held[:early] + swapped[:early])
     in_weights, out_weights, stats = local_weights(
-        part, late_features, held[-1], swapped[-1], inliers, outliers,
+        part, late_features, held[early:] + swapped[early:], inliers, outliers,
         inlier_counts.reshape(1, -1), outlier_counts.reshape(1, -1),
     )
     whole = stats

time: 77.1 us -> 73.9 us (0.958)
  Pallas kernels: 22.8 us -> 17.6 us
  starting transfers between devices: 26.9 us -> 28.1 us
  local copies, waits for them, and re-layouts: 1.75 us -> 2.64 us
    pallas_call x3, Pallas kernels: 6.99 us -> 4.05 us  [the longest x2 2.79 us: outer(): pl.pallas_call(outer_kernel, out_shape=(jax.ShapeDtypeStruct((f // 2, wid...]
    pallas_call x4, Pallas kernels: 7.38 us -> 5.01 us  [weigh(): pl.pallas_call(weigh_kernel, out_shape=jax.ShapeDtypeStruct((q, width), F...]
    unnamed x16, local copies, waits for them, and re-layouts: 1.63 us -> 2.52 us
  transfers between devices with their start and end apart: 20 -> 20, of which waited for: 11 -> 12; matrix products, arithmetic and copies ran while one was open for 1% -> 1% of each run, Pallas kernels for 17% -> 12%
where the time goes in v4:
time: 73.9 us; the launch traced here: 73.7 us
  starting transfers between devices  28.1 us (38%)
  waiting for transfers between devices  22.9 us (31%)
  Pallas kernels  17.6 us (24%)
  local copies, waits for them, and re-layouts  2.64 us (4%)
  other arithmetic  1.68 us (2%)
  between operations  0.9 us (1%)
    ppermute x16, waiting for transfers between devices, cls_swap(): lax.ppermute(value, 'cls', [(i, i ^ 1 << bit_of[i & 1]) for i in range(n)])  18.8 us
    ppermute x16, starting transfers between devices, cls_swap(): lax.ppermute(value, 'cls', [(i, i ^ 1 << bit_of[i & 1]) for i in range(n)])  17.4 us
    ppermute x4, starting transfers between devices, batch_swap(): return lax.ppermute(value, ('cls', 'batch'), pairs)  10.7 us
    pallas_call x1, Pallas kernels, local_weights(): pl.pallas_call(score_kernel, out_shape=(jax.ShapeDtypeStruct((q, ins), BF...  7.23 us
    pallas_call x4, Pallas kernels, weigh(): pl.pallas_call(weigh_kernel, out_shape=jax.ShapeDtypeStruct((q, width), F...  5.01 us
    ppermute x4, waiting for transfers between devices, batch_swap(): return lax.ppermute(value, ('cls', 'batch'), pairs)  4.02 us
    pallas_call x2, Pallas kernels, outer(): pl.pallas_call(outer_kernel, out_shape=(jax.ShapeDtypeStruct((f // 2, wid...  2.79 us
    unnamed x16, local copies, waits for them, and re-layouts  2.52 us
  transfers between devices with their start and end apart: 20, of which 12 were waited for; matrix products, arithmetic and copies ran while one was open for 1% of the time, Pallas kernels for 12%

profile of v4, /device:TPU:0, one launch (start us, length us, event | category | flops | bytes accessed | tf_op | source)
XLA Modules:
  0.0 73.7 jit_solution(2118529713558176442)
XLA Ops:
  0.6 3.0 %collective-permute-start = (bf16[128,1024]{1,0:T(8,128)(2,1)}, bf16[128,1024]{1,0:T(8,128)(2,1)S(1)}, u32[]{:S(2)}, u32[]{:S(2)}) collective-permute-start(bf16[128,1024]{1,0:T(8,128)(2,1)} %refs_0_.1), channel_id=1, source_target_pairs={{0,8},{4,20},{8,0},{12,28},{16,24},{20,4},{24,16},{28,12},{1,9},{5... | collective-permute-start | bytes 786440 | tf_op jit(solution)/shard_map/ppermute | solution.py:43
  3.7 1.5 %collective-permute-start.3 = (bf16[128,1024]{1,0:T(8,128)(2,1)}, bf16[128,1024]{1,0:T(8,128)(2,1)S(1)}, u32[]{:S(2)}, u32[]{:S(2)}) collective-permute-start(bf16[128,1024]{1,0:T(8,128)(2,1)} %refs_0_.1), channel_id=1, source_target_pairs={{0,16},{4,12},{8,24},{12,4},{16,0},{20,28},{24,8},{28,20},{1,17},{... | collective-permute-start | bytes 786440 | tf_op jit(solution)/shard_map/ppermute | solution.py:43
  5.2 5.4 %collective-permute-done.refs_1_ = bf16[128,1024]{1,0:T(8,128)(2,1)S(1)} collective-permute-done((bf16[128,1024]{1,0:T(8,128)(2,1)}, bf16[128,1024]{1,0:T(8,128)(2,1)S(1)}, u32[]{:S(2)}, u32[]{:S(2)}) %collective-permute-start) | collective-permute-done | bytes 262176 | tf_op jit(solution)/shard_map/ppermute | solution.py:43
  10.6 1.5 %collective-permute-start.4 = (bf16[128,1024]{1,0:T(8,128)(2,1)S(1)}, bf16[128,1024]{1,0:T(8,128)(2,1)S(1)}, u32[]{:S(2)}, u32[]{:S(2)}) collective-permute-start(bf16[128,1024]{1,0:T(8,128)(2,1)S(1)} %collective-permute-done.refs_1_), channel_id=1, source_target_pairs={{0,16},{4,12},{8,24},{12,4},{16,0},{20,28},{24,8},{28,20},{1,17},{... | collective-permute-start | bytes 786440 | tf_op jit(solution)/shard_map/ppermute | solution.py:43
  12.0 0.5 collective-permute-start.2
  12.5 4.4 %collective-permute-done.4.refs_1_ = bf16[128,1024]{1,0:T(8,128)(2,1)S(1)} collective-permute-done((bf16[128,1024]{1,0:T(8,128)(2,1)S(1)}, bf16[128,1024]{1,0:T(8,128)(2,1)S(1)}, u32[]{:S(2)}, u32[]{:S(2)}) %collective-permute-start.4) | collective-permute-done | bytes 262176 | tf_op jit(solution)/shard_map/ppermute | solution.py:43
  16.9 1.6 %copy-done.2 = bf16[1024,1024]{1,0:T(8,128)(2,1)S(1)} copy-done((bf16[1024,1024]{1,0:T(8,128)(2,1)S(1)}, bf16[1024,1024]{1,0:T(8,128)(2,1)}, u32[]{:S(2)}) %copy-start.2) | copy-done | bytes 2097176
  18.5 1.3 %arrange.1 = (bf16[1024,1024]{1,0:T(8,128)(2,1)S(1)}, bf16[1024,512]{1,0:T(8,128)(2,1)S(1)}, bf16[1024,512]{1,0:T(8,128)(2,1)S(1)}) custom-call(s32[1]{0:T(128)} %bitcast.me_ref, bf16[1024,1024]{1,0:T(8,128)(2,1)S(1)} %copy-done.2), custom_call_target="tpu_custom_call" | custom-call | bytes 8388608 | tf_op jit(solution)/shard_map/arrange/pallas_call | solution.py:73
  19.9 0.0 copy-start.4
  19.9 1.3 %early.1.part_ref = f32[1024,1024]{1,0:T(8,128)S(1)} custom-call(bf16[1024,512]{1,0:T(8,128)(2,1)S(1)} %get-tuple-element.12.features_ref, bf16[128,1024]{1,0:T(8,128)(2,1)S(1)} %copy-done.3, bf16[128,1024]{1,0:T(8,128)(2,1)S(1)} %collective-permute-done.refs_1_, bf16[128,1024]{1,0:T(8,128)(2,1)S(1)} %collective-permute-done.1.refs_2_, ...), custom_call_target="tpu_custom_call" | custom-call | flops 1073741824 | bytes 4194304 | tf_op jit(solution)/shard_map/early/pallas_call | solution.py:105
  21.2 0.3 copy-done
  21.5 0.6 copy-done.1
  22.1 7.2 %scores.1 = (bf16[1024,1024]{1,0:T(8,128)(2,1)S(1)}, bf16[1024,1024]{1,0:T(8,128)(2,1)S(1)}, f32[4,1024]{1,0:T(4,128)S(1)}) custom-call(f32[1024,1024]{1,0:T(8,128)S(1)} %early.1.part_ref, bf16[1024,512]{1,0:T(8,128)(2,1)S(1)} %get-tuple-element.13.features_ref, bf16[1024,1024]{1,0:T(8,128)(2,1)S(1)} %copy-done, bf16[1024,1024]{1,0:T(8,128)(2,1)S(1)} %copy-done.1, ...), custom_call_target="tpu_custom_call" | custom-call | flops 4294967296 | bytes 4194304 | tf_op jit(solution)/shard_map/scores/pallas_call | solution.py:157
  29.3 0.6 collective-permute-start.7
  29.9 0.8 %collective-permute-done.7 = f32[4,1024]{1,0:T(4,128)S(1)} collective-permute-done((f32[4,1024]{1,0:T(4,128)S(1)}, f32[4,1024]{1,0:T(4,128)S(1)}, u32[]{:S(2)}, u32[]{:S(2)}) %collective-permute-start.7) | collective-permute-done | bytes 16416 | tf_op jit(solution)/shard_map/ppermute | solution.py:43
  30.8 2.4 %collective-permute-start.8 = (f32[4,1024]{1,0:T(4,128)S(1)}, f32[4,1024]{1,0:T(4,128)S(1)}, u32[]{:S(2)}, u32[]{:S(2)}) collective-permute-start(f32[4,1024]{1,0:T(4,128)S(1)} %pad_maximum_fusion.1), channel_id=1, source_target_pairs={{0,8},{4,12},{8,0},{12,4},{16,24},{20,28},{24,16},{28,20},{1,9},{5... | collective-permute-start | bytes 49160 | tf_op jit(solution)/shard_map/ppermute | solution.py:43
  33.3 1.2 %weigh.4.in_ref = f32[1024,512]{1,0:T(8,128)S(1)} custom-call(bf16[1024,1024]{1,0:T(8,128)(2,1)S(1)} %get-tuple-element.15.weights_ref, bf16[1024,1024]{1,0:T(8,128)(2,1)S(1)} %copy-done), custom_call_target="tpu_custom_call" | custom-call | flops 1073741824 | bytes 2097152 | tf_op jit(solution)/shard_map/weigh/pallas_call | solution.py:202
  34.5 0.5 collective-permute-done.8
  35.0 1.2 %collective-permute-start.9 = (f32[4,1024]{1,0:T(4,128)S(1)}, f32[4,1024]{1,0:T(4,128)S(1)}, u32[]{:S(2)}, u32[]{:S(2)}) collective-permute-start(f32[4,1024]{1,0:T(4,128)S(1)} %pad_maximum_fusion.2), channel_id=1, source_target_pairs={{0,16},{4,20},{8,24},{12,28},{16,0},{20,4},{24,8},{28,12},{1,17},{... | collective-permute-start | bytes 49160 | tf_op jit(solution)/shard_map/ppermute | solution.py:43
  36.2 1.2 %weigh.5.out_ref = f32[1024,512]{1,0:T(8,128)S(1)} custom-call(bf16[1024,1024]{1,0:T(8,128)(2,1)S(1)} %get-tuple-element.16.weights_ref, bf16[1024,1024]{1,0:T(8,128)(2,1)S(1)} %copy-done.1), custom_call_target="tpu_custom_call" | custom-call | flops 1073741824 | bytes 2097152 | tf_op jit(solution)/shard_map/weigh/pallas_call | solution.py:202
  37.5 1.4 %collective-permute-done.9 = f32[4,1024]{1,0:T(4,128)S(1)} collective-permute-done((f32[4,1024]{1,0:T(4,128)S(1)}, f32[4,1024]{1,0:T(4,128)S(1)}, u32[]{:S(2)}, u32[]{:S(2)}) %collective-permute-start.9) | collective-permute-done | bytes 16416 | tf_op jit(solution)/shard_map/ppermute | solution.py:43
  38.9 0.0 copy-start.7
  39.0 1.4 %outer.2 = (bf16[512,512]{1,0:T(8,128)(2,1)S(1)}, f32[512,512]{1,0:T(8,128)S(1)}) custom-call(f32[2,1024]{1,0:T(2,128)S(1)} %pad_maximum_fusion.3.scale_ref, f32[1024,512]{1,0:T(8,128)S(1)} %weigh.4.in_ref, f32[1024,512]{1,0:T(8,128)S(1)} %weigh.5.out_ref, bf16[1024,1024]{1,0:T(8,128)(2,1)S(1)} %get-tuple-element.17.turned_ref), custom_call_target="tpu_custom_call" | custom-call | flops 1073741824 | bytes 4194304 | tf_op jit(solution)/shard_map/outer/pallas_call | solution.py:234
  40.4 0.1 collective-permute-start.10
  40.5 1.3 %weigh.6.in_ref = f32[1024,512]{1,0:T(8,128)S(1)} custom-call(bf16[1024,1024]{1,0:T(8,128)(2,1)S(1)} %get-tuple-element.15.weights_ref, bf16[1024,1024]{1,0:T(8,128)(2,1)S(1)} %copy-done), custom_call_target="tpu_custom_call" | custom-call | flops 1073741824 | bytes 2097152 | tf_op jit(solution)/shard_map/weigh/pallas_call | solution.py:202
  41.7 1.3 %weigh.7.out_ref = f32[1024,512]{1,0:T(8,128)S(1)} custom-call(bf16[1024,1024]{1,0:T(8,128)(2,1)S(1)} %get-tuple-element.16.weights_ref, bf16[1024,1024]{1,0:T(8,128)(2,1)S(1)} %copy-done.1), custom_call_target="tpu_custom_call" | custom-call | flops 1073741824 | bytes 2097152 | tf_op jit(solution)/shard_map/weigh/pallas_call | solution.py:202
  43.0 1.4 %outer.3 = (bf16[512,512]{1,0:T(8,128)(2,1)S(1)}, f32[512,512]{1,0:T(8,128)S(1)}) custom-call(f32[2,1024]{1,0:T(2,128)S(1)} %pad_maximum_fusion.3.scale_ref, f32[1024,512]{1,0:T(8,128)S(1)} %weigh.6.in_ref, f32[1024,512]{1,0:T(8,128)S(1)} %weigh.7.out_ref, bf16[1024,1024]{1,0:T(8,128)(2,1)S(1)} %get-tuple-element.17.turned_ref), custom_call_target="tpu_custom_call" | custom-call | flops 1073741824 | bytes 4194304 | tf_op jit(solution)/shard_map/outer/pallas_call | solution.py:234
  44.4 0.6 collective-permute-start.15
  45.0 0.2 convert_add_fusion.1
  45.2 2.1 %collective-permute-start.11 = (bf16[256,512]{1,0:T(8,128)(2,1)S(1)}, bf16[256,512]{1,0:T(8,128)(2,1)S(1)}, u32[]{:S(2)}, u32[]{:S(2)}) collective-permute-start(bf16[256,512]{1,0:T(8,128)(2,1)S(1)} %slice.165), channel_id=1, source_target_pairs={{0,8},{4,20},{8,0},{12,28},{16,24},{20,4},{24,16},{28,12},{1,9},{5... | collective-permute-start | bytes 786440 | tf_op jit(solution)/shard_map/ppermute | solution.py:43
  47.3 0.2 convert_add_fusion
  47.5 1.3 %collective-permute-start.16 = (bf16[256,512]{1,0:T(8,128)(2,1)S(1)}, bf16[256,512]{1,0:T(8,128)(2,1)S(1)}, u32[]{:S(2)}, u32[]{:S(2)}) collective-permute-start(bf16[256,512]{1,0:T(8,128)(2,1)S(1)} %slice.164), channel_id=1, source_target_pairs={{0,8},{4,20},{8,0},{12,28},{16,24},{20,4},{24,16},{28,12},{1,9},{5... | collective-permute-start | bytes 786440 | tf_op jit(solution)/shard_map/ppermute | solution.py:43
  48.8 2.8 %collective-permute-done.11 = bf16[256,512]{1,0:T(8,128)(2,1)S(1)} collective-permute-done((bf16[256,512]{1,0:T(8,128)(2,1)S(1)}, bf16[256,512]{1,0:T(8,128)(2,1)S(1)}, u32[]{:S(2)}, u32[]{:S(2)}) %collective-permute-start.11) | collective-permute-done | bytes 262176 | tf_op jit(solution)/shard_map/ppermute | solution.py:43
  51.6 0.1 slice_add_fusion.1
  51.7 1.2 %collective-permute-start.12 = (bf16[128,512]{1,0:T(8,128)(2,1)S(1)}, bf16[128,512]{1,0:T(8,128)(2,1)S(1)}, u32[]{:S(2)}, u32[]{:S(2)}) collective-permute-start(bf16[128,512]{1,0:T(8,128)(2,1)S(1)} %slice.167), channel_id=1, source_target_pairs={{0,16},{4,12},{8,24},{12,4},{16,0},{20,28},{24,8},{28,20},{1,17},{... | collective-permute-start | bytes 393224 | tf_op jit(solution)/shard_map/ppermute | solution.py:43
  52.9 2.1 %collective-permute-done.16 = bf16[256,512]{1,0:T(8,128)(2,1)S(1)} collective-permute-done((bf16[256,512]{1,0:T(8,128)(2,1)S(1)}, bf16[256,512]{1,0:T(8,128)(2,1)S(1)}, u32[]{:S(2)}, u32[]{:S(2)}) %collective-permute-start.16) | collective-permute-done | bytes 262176 | tf_op jit(solution)/shard_map/ppermute | solution.py:43
  55.0 0.1 slice_add_fusion
  55.1 1.4 %collective-permute-start.17 = (bf16[128,512]{1,0:T(8,128)(2,1)S(1)}, bf16[128,512]{1,0:T(8,128)(2,1)S(1)}, u32[]{:S(2)}, u32[]{:S(2)}) collective-permute-start(bf16[128,512]{1,0:T(8,128)(2,1)S(1)} %slice.166), channel_id=1, source_target_pairs={{0,16},{4,12},{8,24},{12,4},{16,0},{20,28},{24,8},{28,20},{1,17},{... | collective-permute-start | bytes 393224 | tf_op jit(solution)/shard_map/ppermute | solution.py:43
  56.6 0.2 collective-permute-done.12
  56.8 2.2 %collective-permute-start.13 = (bf16[128,512]{1,0:T(8,128)(2,1)S(1)}, bf16[128,512]{1,0:T(8,128)(2,1)S(1)}, u32[]{:S(2)}, u32[]{:S(2)}) collective-permute-start(bf16[128,512]{1,0:T(8,128)(2,1)S(1)} %fusion.1), channel_id=1, source_target_pairs={{0,1},{1,0},{2,3},{3,2},{4,6},{5,7},{6,4},{7,5},{8,9},{9,8},{10,11... | collective-permute-start | bytes 393224 | tf_op jit(solution)/shard_map/ppermute | solution.py:51
  58.9 1.2 %collective-permute-done.17 = bf16[128,512]{1,0:T(8,128)(2,1)S(1)} collective-permute-done((bf16[128,512]{1,0:T(8,128)(2,1)S(1)}, bf16[128,512]{1,0:T(8,128)(2,1)S(1)}, u32[]{:S(2)}, u32[]{:S(2)}) %collective-permute-start.17) | collective-permute-done | bytes 131104 | tf_op jit(solution)/shard_map/ppermute | solution.py:43
  60.2 2.4 %collective-permute-start.18 = (bf16[128,512]{1,0:T(8,128)(2,1)S(1)}, bf16[128,512]{1,0:T(8,128)(2,1)S(1)}, u32[]{:S(2)}, u32[]{:S(2)}) collective-permute-start(bf16[128,512]{1,0:T(8,128)(2,1)S(1)} %fusion), channel_id=1, source_target_pairs={{0,1},{1,0},{2,3},{3,2},{4,6},{5,7},{6,4},{7,5},{8,9},{9,8},{10,11... | collective-permute-start | bytes 393224 | tf_op jit(solution)/shard_map/ppermute | solution.py:51
  62.6 0.2 collective-permute-done.13
  62.9 3.1 %collective-permute-start.14 = (bf16[128,512]{1,0:T(8,128)(2,1)S(1)}, bf16[128,512]{1,0:T(8,128)(2,1)S(1)}, u32[]{:S(2)}, u32[]{:S(2)}) collective-permute-start(bf16[128,512]{1,0:T(8,128)(2,1)S(1)} %add_convert_fusion.1), channel_id=1, source_target_pairs={{0,2},{1,3},{2,0},{3,1},{4,5},{5,4},{6,7},{7,6},{8,10},{9,11},{10,... | collective-permute-start | bytes 393224 | tf_op jit(solution)/shard_map/ppermute | solution.py:51
  65.9 0.7 collective-permute-done.18
  66.6 3.0 %collective-permute-start.19 = (bf16[128,512]{1,0:T(8,128)(2,1)S(1)}, bf16[128,512]{1,0:T(8,128)(2,1)S(1)}, u32[]{:S(2)}, u32[]{:S(2)}) collective-permute-start(bf16[128,512]{1,0:T(8,128)(2,1)S(1)} %add_convert_fusion), channel_id=1, source_target_pairs={{0,2},{1,3},{2,0},{3,1},{4,5},{5,4},{6,7},{7,6},{8,10},{9,11},{10,... | collective-permute-start | bytes 393224 | tf_op jit(solution)/shard_map/ppermute | solution.py:51
  69.7 3.1 %collective-permute-done.19 = bf16[128,512]{1,0:T(8,128)(2,1)S(1)} collective-permute-done((bf16[128,512]{1,0:T(8,128)(2,1)S(1)}, bf16[128,512]{1,0:T(8,128)(2,1)S(1)}, u32[]{:S(2)}, u32[]{:S(2)}) %collective-permute-start.19) | collective-permute-done | bytes 131104 | tf_op jit(solution)/shard_map/ppermute | solution.py:51
  72.9 0.8 %pad_maximum_fusion = f32[128,1024]{1,0:T(8,128)} fusion(f32[128,512]{1,0:T(8,128)S(1)} %convert_add_fusion.2, f32[128,512]{1,0:T(8,128)S(1)} %convert_add_fusion.3), kind=kLoop, calls=%fused_computation.6 | loop fusion | flops 131072 | bytes 1048576 | tf_op jit(solution)/shard_map/concatenate | solution.py:307
  (40 shorter events, 0.6 us)
Async XLA Ops:
  0.6 9.9 %collective-permute-start = (bf16[128,1024]{1,0:T(8,128)(2,1)}, bf16[128,1024]{1,0:T(8,128)(2,1)S(1)}, u32[]{:S(2)}, u32[]{:S(2)}) collective-permute-start(bf16[128,1024]{1,0:T(8,128)(2,1)} %refs_0_.1), channel_id=1, source_target_pairs={{0,8},{4,20},{8,0},{12,28},{16,24},{20,4},{24,16},{28,12},{1,9},{5... | collective-permute-start | bytes 786440 | tf_op jit(solution)/shard_map/ppermute | solution.py:43
  3.7 8.9 %collective-permute-start.3 = (bf16[128,1024]{1,0:T(8,128)(2,1)}, bf16[128,1024]{1,0:T(8,128)(2,1)S(1)}, u32[]{:S(2)}, u32[]{:S(2)}) collective-permute-start(bf16[128,1024]{1,0:T(8,128)(2,1)} %refs_0_.1), channel_id=1, source_target_pairs={{0,16},{4,12},{8,24},{12,4},{16,0},{20,28},{24,8},{28,20},{1,17},{... | collective-permute-start | bytes 786440 | tf_op jit(solution)/shard_map/ppermute | solution.py:43
  10.6 6.4 %collective-permute-start.4 = (bf16[128,1024]{1,0:T(8,128)(2,1)S(1)}, bf16[128,1024]{1,0:T(8,128)(2,1)S(1)}, u32[]{:S(2)}, u32[]{:S(2)}) collective-permute-start(bf16[128,1024]{1,0:T(8,128)(2,1)S(1)} %collective-permute-done.refs_1_), channel_id=1, source_target_pairs={{0,16},{4,12},{8,24},{12,4},{16,0},{20,28},{24,8},{28,20},{1,17},{... | collective-permute-start | bytes 786440 | tf_op jit(solution)/shard_map/ppermute | solution.py:43
  12.0 7.8 %collective-permute-start.1 = (bf16[128,1024]{1,0:T(8,128)(2,1)}, bf16[128,1024]{1,0:T(8,128)(2,1)S(1)}, u32[]{:S(2)}, u32[]{:S(2)}) collective-permute-start(bf16[128,1024]{1,0:T(8,128)(2,1)} %refs_0_.1), channel_id=1, source_target_pairs={{0,4},{4,0},{8,12},{12,8},{16,20},{20,16},{24,28},{28,24},{1,5},{5... | collective-permute-start | bytes 786440 | tf_op jit(solution)/shard_map/ppermute | solution.py:43
  12.0 7.8 %collective-permute-start.2 = (bf16[128,1024]{1,0:T(8,128)(2,1)S(1)}, bf16[128,1024]{1,0:T(8,128)(2,1)S(1)}, u32[]{:S(2)}, u32[]{:S(2)}) collective-permute-start(bf16[128,1024]{1,0:T(8,128)(2,1)S(1)} %collective-permute-done.refs_1_), channel_id=1, source_target_pairs={{0,4},{4,0},{8,12},{12,8},{16,20},{20,16},{24,28},{28,24},{1,5},{5... | collective-permute-start | bytes 786440 | tf_op jit(solution)/shard_map/ppermute | solution.py:43
  12.5 8.6 %collective-permute-start.5 = (bf16[128,1024]{1,0:T(8,128)(2,1)S(1)}, bf16[128,1024]{1,0:T(8,128)(2,1)S(1)}, u32[]{:S(2)}, u32[]{:S(2)}) collective-permute-start(bf16[128,1024]{1,0:T(8,128)(2,1)S(1)} %collective-permute-done.3.refs_0_), channel_id=1, source_target_pairs={{0,4},{4,0},{8,12},{12,8},{16,20},{20,16},{24,28},{28,24},{1,5},{5... | collective-permute-start | bytes 786440 | tf_op jit(solution)/shard_map/ppermute | solution.py:43
  16.9 4.2 %collective-permute-start.6 = (bf16[128,1024]{1,0:T(8,128)(2,1)S(1)}, bf16[128,1024]{1,0:T(8,128)(2,1)S(1)}, u32[]{:S(2)}, u32[]{:S(2)}) collective-permute-start(bf16[128,1024]{1,0:T(8,128)(2,1)S(1)} %collective-permute-done.4.refs_1_), channel_id=1, source_target_pairs={{0,4},{4,0},{8,12},{12,8},{16,20},{20,16},{24,28},{28,24},{1,5},{5... | collective-permute-start | bytes 786440 | tf_op jit(solution)/shard_map/ppermute | solution.py:43
  16.9 1.6 %copy-start.2 = (bf16[1024,1024]{1,0:T(8,128)(2,1)S(1)}, bf16[1024,1024]{1,0:T(8,128)(2,1)}, u32[]{:S(2)}) copy-start(bf16[1024,1024]{1,0:T(8,128)(2,1)} %features_ref.1) | copy-start | bytes 6291460
  18.5 1.3 %copy-start.3 = (bf16[128,1024]{1,0:T(8,128)(2,1)S(1)}, bf16[128,1024]{1,0:T(8,128)(2,1)}, u32[]{:S(2)}) copy-start(bf16[128,1024]{1,0:T(8,128)(2,1)} %refs_0_.1) | copy-start | bytes 786436
  19.9 1.6 %copy-start = (bf16[1024,1024]{1,0:T(8,128)(2,1)S(1)}, bf16[1024,1024]{1,0:T(8,128)(2,1)}, u32[]{:S(2)}) copy-start(bf16[1024,1024]{1,0:T(8,128)(2,1)} %patterns_ref.6) | copy-start | bytes 6291460
  19.9 2.2 %copy-start.1 = (bf16[1024,1024]{1,0:T(8,128)(2,1)S(1)}, bf16[1024,1024]{1,0:T(8,128)(2,1)}, u32[]{:S(2)}) copy-start(bf16[1024,1024]{1,0:T(8,128)(2,1)} %patterns_ref.7) | copy-start | bytes 6291460
  19.9 2.2 %copy-start.4 = (s32[1024]{0:T(1024)S(1)}, s32[1024]{0:T(1024)}, u32[]{:S(2)}) copy-start(s32[1024]{0:T(1024)} %param.11) | copy-start | bytes 12292
  19.9 2.2 %copy-start.5 = (s32[1024]{0:T(1024)S(1)}, s32[1024]{0:T(1024)}, u32[]{:S(2)}) copy-start(s32[1024]{0:T(1024)} %param.12) | copy-start | bytes 12292
  29.3 1.4 %collective-permute-start.7 = (f32[4,1024]{1,0:T(4,128)S(1)}, f32[4,1024]{1,0:T(4,128)S(1)}, u32[]{:S(2)}, u32[]{:S(2)}) collective-permute-start(f32[4,1024]{1,0:T(4,128)S(1)} %get-tuple-element.14), channel_id=1, source_target_pairs={{0,4},{4,0},{8,12},{12,8},{16,20},{20,16},{24,28},{28,24},{1,5},{5... | collective-permute-start | bytes 49160 | tf_op jit(solution)/shard_map/ppermute | solution.py:43
  30.8 4.2 %collective-permute-start.8 = (f32[4,1024]{1,0:T(4,128)S(1)}, f32[4,1024]{1,0:T(4,128)S(1)}, u32[]{:S(2)}, u32[]{:S(2)}) collective-permute-start(f32[4,1024]{1,0:T(4,128)S(1)} %pad_maximum_fusion.1), channel_id=1, source_target_pairs={{0,8},{4,12},{8,0},{12,4},{16,24},{20,28},{24,16},{28,20},{1,9},{5... | collective-permute-start | bytes 49160 | tf_op jit(solution)/shard_map/ppermute | solution.py:43
  35.0 3.8 %collective-permute-start.9 = (f32[4,1024]{1,0:T(4,128)S(1)}, f32[4,1024]{1,0:T(4,128)S(1)}, u32[]{:S(2)}, u32[]{:S(2)}) collective-permute-start(f32[4,1024]{1,0:T(4,128)S(1)} %pad_maximum_fusion.2), channel_id=1, source_target_pairs={{0,16},{4,20},{8,24},{12,28},{16,0},{20,4},{24,8},{28,12},{1,17},{... | collective-permute-start | bytes 49160 | tf_op jit(solution)/shard_map/ppermute | solution.py:43
  36.2 2.7 %copy-start.6 = (s32[1024]{0:T(1024)S(1)}, s32[1024]{0:T(1024)}, u32[]{:S(2)}) copy-start(s32[1024]{0:T(1024)} %param.13) | copy-start | bytes 12292
  38.9 1.5 %copy-start.7 = (f32[1024]{0:T(1024)}, f32[1024]{0:T(1024)S(1)}, u32[]{:S(2)}) copy-start(f32[1024]{0:T(1024)S(1)} %get-tuple-element.23) | copy-start | bytes 12292
  40.4 4.6 %collective-permute-start.10 = (bf16[512,512]{1,0:T(8,128)(2,1)S(1)}, bf16[512,512]{1,0:T(8,128)(2,1)S(1)}, u32[]{:S(2)}, u32[]{:S(2)}) collective-permute-start(bf16[512,512]{1,0:T(8,128)(2,1)S(1)} %get-tuple-element.19), channel_id=1, source_target_pairs={{0,4},{4,0},{8,12},{12,8},{16,20},{20,16},{24,28},{28,24},{1,5},{5... | collective-permute-start | bytes 1572872 | tf_op jit(solution)/shard_map/ppermute | solution.py:43
  44.4 2.9 %collective-permute-start.15 = (bf16[512,512]{1,0:T(8,128)(2,1)S(1)}, bf16[512,512]{1,0:T(8,128)(2,1)S(1)}, u32[]{:S(2)}, u32[]{:S(2)}) collective-permute-start(bf16[512,512]{1,0:T(8,128)(2,1)S(1)} %get-tuple-element.21), channel_id=1, source_target_pairs={{0,4},{4,0},{8,12},{12,8},{16,20},{20,16},{24,28},{28,24},{1,5},{5... | collective-permute-start | bytes 1572872 | tf_op jit(solution)/shard_map/ppermute | solution.py:43
  45.2 6.4 %collective-permute-start.11 = (bf16[256,512]{1,0:T(8,128)(2,1)S(1)}, bf16[256,512]{1,0:T(8,128)(2,1)S(1)}, u32[]{:S(2)}, u32[]{:S(2)}) collective-permute-start(bf16[256,512]{1,0:T(8,128)(2,1)S(1)} %slice.165), channel_id=1, source_target_pairs={{0,8},{4,20},{8,0},{12,28},{16,24},{20,4},{24,16},{28,12},{1,9},{5... | collective-permute-start | bytes 786440 | tf_op jit(solution)/shard_map/ppermute | solution.py:43
  47.5 7.5 %collective-permute-start.16 = (bf16[256,512]{1,0:T(8,128)(2,1)S(1)}, bf16[256,512]{1,0:T(8,128)(2,1)S(1)}, u32[]{:S(2)}, u32[]{:S(2)}) collective-permute-start(bf16[256,512]{1,0:T(8,128)(2,1)S(1)} %slice.164), channel_id=1, source_target_pairs={{0,8},{4,20},{8,0},{12,28},{16,24},{20,4},{24,16},{28,12},{1,9},{5... | collective-permute-start | bytes 786440 | tf_op jit(solution)/shard_map/ppermute | solution.py:43
  51.7 5.0 %collective-permute-start.12 = (bf16[128,512]{1,0:T(8,128)(2,1)S(1)}, bf16[128,512]{1,0:T(8,128)(2,1)S(1)}, u32[]{:S(2)}, u32[]{:S(2)}) collective-permute-start(bf16[128,512]{1,0:T(8,128)(2,1)S(1)} %slice.167), channel_id=1, source_target_pairs={{0,16},{4,12},{8,24},{12,4},{16,0},{20,28},{24,8},{28,20},{1,17},{... | collective-permute-start | bytes 393224 | tf_op jit(solution)/shard_map/ppermute | solution.py:43
  55.1 5.0 %collective-permute-start.17 = (bf16[128,512]{1,0:T(8,128)(2,1)S(1)}, bf16[128,512]{1,0:T(8,128)(2,1)S(1)}, u32[]{:S(2)}, u32[]{:S(2)}) collective-permute-start(bf16[128,512]{1,0:T(8,128)(2,1)S(1)} %slice.166), channel_id=1, source_target_pairs={{0,16},{4,12},{8,24},{12,4},{16,0},{20,28},{24,8},{28,20},{1,17},{... | collective-permute-start | bytes 393224 | tf_op jit(solution)/shard_map/ppermute | solution.py:43
  56.8 6.1 %collective-permute-start.13 = (bf16[128,512]{1,0:T(8,128)(2,1)S(1)}, bf16[128,512]{1,0:T(8,128)(2,1)S(1)}, u32[]{:S(2)}, u32[]{:S(2)}) collective-permute-start(bf16[128,512]{1,0:T(8,128)(2,1)S(1)} %fusion.1), channel_id=1, source_target_pairs={{0,1},{1,0},{2,3},{3,2},{4,6},{5,7},{6,4},{7,5},{8,9},{9,8},{10,11... | collective-permute-start | bytes 393224 | tf_op jit(solution)/shard_map/ppermute | solution.py:51
  60.2 6.4 %collective-permute-start.18 = (bf16[128,512]{1,0:T(8,128)(2,1)S(1)}, bf16[128,512]{1,0:T(8,128)(2,1)S(1)}, u32[]{:S(2)}, u32[]{:S(2)}) collective-permute-start(bf16[128,512]{1,0:T(8,128)(2,1)S(1)} %fusion), channel_id=1, source_target_pairs={{0,1},{1,0},{2,3},{3,2},{4,6},{5,7},{6,4},{7,5},{8,9},{9,8},{10,11... | collective-permute-start | bytes 393224 | tf_op jit(solution)/shard_map/ppermute | solution.py:51
  62.9 6.8 %collective-permute-start.14 = (bf16[128,512]{1,0:T(8,128)(2,1)S(1)}, bf16[128,512]{1,0:T(8,128)(2,1)S(1)}, u32[]{:S(2)}, u32[]{:S(2)}) collective-permute-start(bf16[128,512]{1,0:T(8,128)(2,1)S(1)} %add_convert_fusion.1), channel_id=1, source_target_pairs={{0,2},{1,3},{2,0},{3,1},{4,5},{5,4},{6,7},{7,6},{8,10},{9,11},{10,... | collective-permute-start | bytes 393224 | tf_op jit(solution)/shard_map/ppermute | solution.py:51
  66.6 6.2 %collective-permute-start.19 = (bf16[128,512]{1,0:T(8,128)(2,1)S(1)}, bf16[128,512]{1,0:T(8,128)(2,1)S(1)}, u32[]{:S(2)}, u32[]{:S(2)}) collective-permute-start(bf16[128,512]{1,0:T(8,128)(2,1)S(1)} %add_convert_fusion), channel_id=1, source_target_pairs={{0,2},{1,3},{2,0},{3,1},{4,5},{5,4},{6,7},{7,6},{8,10},{9,11},{10,... | collective-permute-start | bytes 393224 | tf_op jit(solution)/shard_map/ppermute | solution.py:51
